TPU v7x, 128 devices: a whole 4x4x4 slice. The times are simulated.
128 devices in a mesh: sky: 32 (over y, z, core), band: 4 (over x).
Axes of the slice: x: 4, y: 4, z: 4, core: 2. Of those that a mesh axis runs over, the one named last changes fastest.
Arguments:
- band_maps: float32 [16, 512, 1024], P('band', 'sky'), may hold values from -64 to 64
- cycle_weight: float32 [512], P('sky'), may hold values from 0.5 to 2
- cycle_len: int32 [512], P('sky'), may hold values from 4 to 1024, as said below
- m_order: int32 [1024], replicated, may hold values from 0 to 1023, each once
- legendre: bfloat16 [1024, 1024, 512], P(('sky', 'band')), may hold values from -4 to 4
- band_start: int32 [1], replicated, may hold values from 256 to 1023
Outputs:
- clean_map: float32 [512, 1024], P('sky', 'band')
Inputs may be any that keep to these rules, and one draw needn't show every extreme that they name: `cycle_len`: each cycle slot holds a polar-cap cycle of 4 i pixels, every i from 1 to 256 on exactly two cycle slots. `m_order`: each azimuthal order 0 to 1023 is served by exactly one order slot.
All inputs are finite; a program needn't handle non-finite values.
Results may differ from a plain program's by a relative error of at most 0.0023.
Values may be sent and summed in bfloat16 or wider, within the bound.
A program may use at most 128 MiB of HBM per device.

v0:
```python
import functools
import math

import jax
import jax.numpy as jnp
from jax import lax
from jax.experimental import pallas as pl
from jax.experimental.pallas import tpu as pltpu
from jax.sharding import PartitionSpec as P

BANDS = 16
M = 1024
LB = 1024
DOM = 4
RIDGE = 0.05
QUARTER = 256
NDEV = 128
BPD = 4
RPD = 16
GROUPS = 2 * BPD
SLOTS = 8
MESH = pl.DeviceIdType.MESH
BF = jnp.bfloat16
F32 = jnp.float32
BACK = jnp.float32
NT = (((1,), (1,)), ((), ()))
NN = (((1,), (0,)), ((), ()))


def mm(a, b, dims, precision=None):
    return lax.dot_general(a, b, dims, precision=precision, preferred_element_type=F32)


def split(x):
    hi = x.astype(BF)
    return hi, (x - hi.astype(F32)).astype(BF)


def trig_tables(order, length):
    pixel = lax.broadcasted_iota(jnp.int32, order.shape, 1)
    turns = order * (2 * pixel + 1).astype(F32)
    lf = jnp.full((1, QUARTER), length, jnp.int32).astype(F32)
    quarter = 0.5 * lf
    count = jnp.floor(turns * (1.0 / quarter) + 0.5)
    y = (turns - count * quarter) * (math.pi / lf)
    z = y * y
    s = ((-1.9515295891e-4 * z + 8.3321608736e-3) * z - 1.6666654611e-1) * z * y + y
    c = ((2.443315711809948e-5 * z - 1.388731625493765e-3) * z + 4.166664568298827e-2) * (z * z) - 0.5 * z + 1.0
    quad = count - 4.0 * jnp.floor(count * 0.25)
    upper = quad >= 2.0
    odd = (quad == 1.0) | (quad == 3.0)
    sin = jnp.where(odd, c, s)
    cos = jnp.where(odd, s, c)
    sin = jnp.where(upper, -sin, sin)
    cos = jnp.where((quad == 1.0) | (quad == 2.0), -cos, cos)
    return cos, sin


def order_rows():
    row = lax.broadcasted_iota(jnp.int32, (32, QUARTER), 0)
    inner = (4 * (row % 8) + row // 8).astype(F32)
    outer = (32 * row).astype(F32)
    return inner, outer


def reversal():
    row = lax.broadcasted_iota(jnp.int32, (QUARTER, QUARTER), 0)
    col = lax.broadcasted_iota(jnp.int32, (QUARTER, QUARTER), 1)
    return jnp.where(row + col == QUARTER - 1, 1.0, 0.0).astype(F32)


def window_taper(window):
    turns = 2.0 * window + 1.0
    count = jnp.floor(turns * (1.0 / LB) + 0.5)
    y = (turns - count * LB) * (math.pi / (2 * LB))
    z = y * y
    s = ((-1.9515295891e-4 * z + 8.3321608736e-3) * z - 1.6666654611e-1) * z * y + y
    c = ((2.443315711809948e-5 * z - 1.388731625493765e-3) * z + 4.166664568298827e-2) * (z * z) - 0.5 * z + 1.0
    return jnp.where(count == 0.0, s, jnp.where(count == 1.0, c, -s))


def swap_blocks(rows, lane_group):
    rows = list(rows)
    for bit in (1, 2, 4):
        low = (lane_group // bit) % 2 == 0
        for i in range(8):
            if i & bit:
                continue
            a, b = rows[i], rows[i + bit]
            rows[i] = jnp.where(low, a, pltpu.roll(b, 16 * bit, 1))
            rows[i + bit] = jnp.where(low, pltpu.roll(a, 128 - 16 * bit, 1), b)
    return rows


def whole_kernel(
    maps_hbm, weight_hbm, len_hbm, order_hbm, order_rows_hbm, leg_hbm, start_hbm, out_ref,
    maps, weight, length_of, order, order_vec, start, leg,
    xs, xr, cs, tp, th, tl, hot, msg, arrived, hx, hy, back, returned, nq, pb, nd, ndb, got, wide, part, parts,
    small_sem, leg_sem, local_sem, send_sem, recv_sem, pix_send, pix_recv, cov_send, cov_recv,
):
    sky = lax.axis_index("sky")
    band = lax.axis_index("band")
    me = sky * 4 + band
    bands = [band] + [lax.rem(band + j, 4) for j in range(1, 4)]
    others = bands[1:]

    small = [
        pltpu.make_async_copy(src, dst, small_sem.at[i])
        for i, (src, dst) in enumerate((
            (maps_hbm, maps), (len_hbm, length_of), (weight_hbm, weight), (order_rows_hbm, order_vec),
            (order_hbm, order), (start_hbm, start),
        ))
    ]
    for copy in small:
        copy.start()
    loads = [pltpu.make_async_copy(leg_hbm.at[i], leg.at[i], leg_sem.at[i]) for i in range(SLOTS)]
    for copy in loads:
        copy.start()

    barrier = pltpu.get_barrier_semaphore()

    def greet(i):
        row = lax.rem(sky + i, 32)
        for column in bands:
            pl.semaphore_signal(barrier, inc=1, device_id=(row, column), device_id_type=MESH)

    for column in others:
        pl.semaphore_signal(barrier, inc=1, device_id=(sky, column), device_id_type=MESH)
    greet(1)

    flip = reversal()
    for copy in small:
        copy.wait()
    for tile in range(8):
        xs[tile] = maps[:, tile * 128:tile * 128 + 128]
    for tile in (8, 9, 10):
        xs[tile] = jnp.zeros((BPD * RPD, 128), F32)
        xr[tile] = jnp.zeros((BPD * RPD, 128), F32)
    for block in range(4):
        turned = mm(maps[:, block * QUARTER:(block + 1) * QUARTER], flip, NN, lax.Precision.HIGHEST)
        xr[6 - 2 * block] = turned[:, 0:128]
        xr[7 - 2 * block] = turned[:, 128:256]
    inner, outer = order_rows()
    lane4 = lax.broadcasted_iota(jnp.int32, (BPD, 128), 1)
    pixel = lax.broadcasted_iota(jnp.int32, (BPD, QUARTER), 1)
    quad_group = lax.broadcasted_iota(jnp.int32, (8, 128), 1) // 32

    def window(ref, r, offset):
        tile = offset // 128
        rest = offset - tile * 128
        shift = lax.rem(128 - rest, 128)
        pieces = [pltpu.roll(ref[tile + i, pl.ds(r, BPD, stride=RPD), :], shift, 1) for i in range(3)]
        keep = lane4 < 128 - rest
        return jnp.concatenate(
            [jnp.where(keep, pieces[0], pieces[1]), jnp.where(keep, pieces[1], pieces[2])], axis=1
        )

    def analyse(r, carry):
        length = length_of[r]
        scale = weight[r] * (1.0 / math.sqrt(512 * 1024))
        inside = pixel < length // 4
        x0 = jnp.concatenate([xs[i, pl.ds(r, BPD, stride=RPD), :] for i in range(2)], axis=1)
        x1 = window(xr, r, 1024 - length // 2)
        x2 = window(xs, r, length // 2)
        x3 = window(xr, r, 1024 - length)
        x0, x1, x2, x3 = [jnp.where(inside, v, 0.0) * scale for v in (x0, x1, x2, x3)]
        even = ((x0 + x3) + (x1 + x2), (x0 + x3) - (x1 + x2))
        odd = ((x0 - x3) - (x1 - x2), (x0 - x3) + (x1 - x2))
        cos_p, sin_p = trig_tables(inner, length)
        cos_q, sin_q = trig_tables(outer, length)
        ch, cl = split(cos_q)
        sh, sl = split(sin_q)
        tp[r, 0:32, :] = cos_p
        tp[r, 32:64, :] = sin_p
        th[r] = jnp.concatenate([ch, sh], axis=1)
        tl[r] = jnp.concatenate([cl, sl], axis=1)
        cqh, cql, sqh, sql = [jnp.concatenate([v] * 4, axis=0) for v in (ch, cl, sh, sl)]

        def rows(pair, table):
            pieces = []
            for b in range(BPD):
                for c in range(4):
                    source = pair[c % 2][b:b + 1]
                    pieces.append(jnp.broadcast_to(source, (8, QUARTER)) * table[c * 8:c * 8 + 8])
            return split(jnp.concatenate(pieces, axis=0))

        ech, ecl = rows(even, cos_p)
        esh, esl = rows(even, -sin_p)
        och, ocl = rows(odd, -cos_p)
        osh, osl = rows(odd, -sin_p)
        right_c = jnp.concatenate([cqh, cql, cqh], axis=1)
        right_s = jnp.concatenate([sqh, sql, sqh], axis=1)
        real = mm(jnp.concatenate([ech, ech, ecl], axis=1), right_c, NT) + mm(
            jnp.concatenate([esh, esh, esl], axis=1), right_s, NT
        )
        imag = mm(jnp.concatenate([och, och, ocl], axis=1), right_s, NT) + mm(
            jnp.concatenate([osh, osh, osl], axis=1), right_c, NT
        )
        for b in range(BPD):
            for half, val in enumerate((real, imag)):
                v = [val[b * 32 + c * 8:b * 32 + c * 8 + 8] for c in range(4)]
                picked = jnp.where(
                    quad_group == 0, v[0], jnp.where(quad_group == 1, v[1], jnp.where(quad_group == 2, v[2], v[3]))
                )
                at = pl.multiple_of(((b * 2 + half) * RPD + r) * 8, 8)
                cs[pl.ds(at, 8), :] = picked
        return carry

    def analyse_four(i, carry):
        for j in range(4):
            analyse(4 * i + j, carry)
        return carry

    lax.fori_loop(2, 32, lambda i, carry: (greet(i), carry)[1], 0)
    lax.fori_loop(0, RPD // 4, analyse_four, 0)

    flat = jnp.concatenate([cs[pl.ds(a, 128, stride=8), :].astype(BF) for a in range(8)], axis=1)
    slots = order_vec[...]
    where_to = (slots % 32 // 4 * 128 + slots % 4 * 32 + slots // 32).astype(F32)
    lane128 = lax.broadcasted_iota(jnp.int32, (128, 128), 1).astype(F32)
    for block in range(8):
        target = jnp.broadcast_to(where_to[block:block + 1], (128, 128)).T
        row_hot = jnp.concatenate(
            [jnp.where(target == lane128 + 128.0 * a, 1.0, 0.0).astype(BF) for a in range(8)], axis=1
        )
        hot[block * 128:block * 128 + 128, :] = row_hot
        moved = mm(row_hot, flat, NT)
        msg[block * 16:block * 16 + 16] = moved.reshape(16, SLOTS, 128).astype(BF)

    own = pltpu.make_async_copy(msg.at[me], arrived.at[me], local_sem)
    own.start()
    pl.semaphore_wait(barrier, NDEV - 1)

    def everyone(src, dst, phase):
        def one(row, column):
            pltpu.make_async_remote_copy(
                src_ref=src.at[row * 4 + column], dst_ref=dst.at[me], send_sem=send_sem.at[phase],
                recv_sem=recv_sem.at[phase], device_id=(row, column), device_id_type=MESH,
            ).start()

        for column in others:
            one(sky, column)

        def rows(i, carry):
            row = lax.rem(sky + i, 32)
            for column in bands:
                one(row, column)
            return carry

        lax.fori_loop(1, 32, rows, 0)
        return pltpu.make_async_remote_copy(
            src_ref=src.at[pl.ds(0, NDEV - 1)], dst_ref=dst.at[pl.ds(0, NDEV - 1)], send_sem=send_sem.at[phase],
            recv_sem=recv_sem.at[phase], device_id=(sky, others[0]), device_id_type=MESH,
        )

    out_copies = everyone(msg, arrived, 0)
    window_at = lax.broadcasted_iota(jnp.int32, (8, LB), 1).astype(F32)
    taper = window_taper(window_at)[0:1] * (1.0 / math.sqrt(LB))
    degree = lax.broadcasted_iota(jnp.int32, (1, LB), 1) + start[0]
    own.wait()
    out_copies.wait_recv()

    lane_group = lax.broadcasted_iota(jnp.int32, (SLOTS, 128), 1) // 16
    for tile in range(4):
        for source in range(4):
            here = [arrived[(tile * 8 + i) * 4 + source].astype(F32) for i in range(8)]
            for g, val in enumerate(swap_blocks(here, lane_group)):
                at = (source * GROUPS + g) * 8
                hx[tile, at:at + 8, :] = val
    for m in range(SLOTS):
        keep = jnp.where(degree >= order[me * SLOTS + m], taper, 0.0)
        coeff = jnp.concatenate(
            [hx[tile, pl.ds(m, 4 * GROUPS, stride=8), :].astype(BF) for tile in range(4)], axis=1
        )
        loads[m].wait()
        table = leg[m]
        harmonic = mm(coeff, table, NT)
        result = mm((harmonic * keep).astype(BF), table, NN)
        for tile in range(4):
            hy[tile, pl.ds(m, 4 * GROUPS, stride=8), :] = result[:, tile * 128:tile * 128 + 128]
    for tile in range(4):
        for source in range(4):
            done = []
            for g in range(GROUPS):
                at = (source * GROUPS + g) * 8
                done.append(hy[tile, at:at + 8, :])
            for i, val in enumerate(swap_blocks(done, lane_group)):
                back[(tile * 8 + i) * 4 + source] = val.astype(back.dtype)

    own_back = pltpu.make_async_copy(back.at[me], returned.at[me], local_sem)
    own_back.start()
    back_copies = everyone(back, returned, 1)
    for i in range(3):
        for tile in range(20):
            if tile not in (8, 9, 10):
                pb[i, tile] = jnp.zeros((BPD, 128), F32)
    flip16 = flip.astype(BF)
    own_back.wait()
    back_copies.wait_recv()

    turned = jnp.concatenate(
        [returned[d * 16:d * 16 + 16].astype(F32).reshape(128, 128).T for d in range(8)], axis=1
    )
    stacked = jnp.concatenate(split(turned), axis=0)
    lane1 = lax.broadcasted_iota(jnp.int32, (128, 128), 1)
    for pair in range(4):
        moved = mm(stacked, hot[:, pair * QUARTER:(pair + 1) * QUARTER], NN)
        natural = (moved[0:128] + moved[128:256]) * (2.0 / math.sqrt(M))
        for half in range(2):
            a = pair * 2 + half
            val = natural[:, half * 128:half * 128 + 128]
            if a == 0:
                val = jnp.where(lane1 == 0, 0.5 * val, val)
            cs[pl.ds(a, 128, stride=8), :] = val

    def synthesise(r, carry):
        cos_p = tp[r, 0:32, :]
        sin_p = tp[r, 32:64, :]
        table_hi = jnp.concatenate([th[r]] * 4, axis=0)
        table_lo = jnp.concatenate([tl[r]] * 4, axis=0)
        pieces = []
        for g in range(GROUPS):
            at = pl.multiple_of((g * RPD + r) * 8, 8)
            v = cs[pl.ds(at, 8), :]
            for c in range(4):
                pieces.append(jnp.where(quad_group == c, v, 0.0))
        hi, lo = split(jnp.concatenate(pieces, axis=0))
        full = mm(jnp.concatenate([hi, lo], axis=1), jnp.concatenate([table_hi, table_hi], axis=0), NN) + mm(
            hi, table_lo, NN
        )
        quarters = [[], [], [], []]
        for b in range(BPD):
            re = full[(2 * b) * 32:(2 * b) * 32 + 32]
            im = full[(2 * b + 1) * 32:(2 * b + 1) * 32 + 32]
            even = cos_p * re[:, :QUARTER] - sin_p * re[:, QUARTER:]
            odd = cos_p * im[:, QUARTER:] + sin_p * im[:, :QUARTER]
            ce, co = even[0:8] + even[16:24], even[8:16] + even[24:32]
            de, do = odd[0:8] + odd[16:24], odd[8:16] + odd[24:32]
            for i, total in enumerate((ce + co - de - do, ce - co + de - do, ce - co - de + do, ce + co + de + do)):
                quarters[i].append(jnp.sum(total, axis=0, keepdims=True))
        inside = pixel < length_of[r] // 4
        for i in range(4):
            val = jnp.where(inside, jnp.concatenate(quarters[i], axis=0), 0.0)
            nq[i, r] = val.astype(BF).astype(F32)
        return carry

    lax.fori_loop(0, RPD, synthesise, 0, unroll=4)
    for i in (1, 3):
        whole = nq[i].reshape(RPD * BPD, QUARTER).astype(BF)
        nq[i] = mm(whole, flip16, NN).reshape(RPD, BPD, QUARTER)

    def place(r, carry):
        length = length_of[r]
        tiles = []
        for i, offset in ((1, length // 2 - QUARTER), (2, length // 2), (3, length - QUARTER)):
            tile = (offset + 1024) // 128 - 8
            rest = offset - tile * 128
            val = nq[i, r]
            low = pltpu.roll(val[:, :128], rest, 1)
            high = pltpu.roll(val[:, 128:], rest, 1)
            wrapped = lane4 < rest
            pb[i - 1, 8] = jnp.where(wrapped, 0.0, low)
            pb[i - 1, 9] = jnp.where(wrapped, low, high)
            pb[i - 1, 10] = jnp.where(wrapped, high, 0.0)
            tiles.append(tile)
        first = nq[0, r]
        for t in range(8):
            total = pb[0, 8 + t - tiles[0]] + pb[1, 8 + t - tiles[1]] + pb[2, 8 + t - tiles[2]]
            if t < 2:
                total = total + first[:, t * 128:t * 128 + 128]
            nd[t, pl.ds(r, BPD, stride=RPD), :] = total
        return carry

    lax.fori_loop(0, RPD, place, 0, unroll=2)
    for t in range(4):
        ndb[t] = jnp.concatenate([nd[2 * t], nd[2 * t + 1]], axis=1).astype(BF)

    own_pixels = pltpu.make_async_copy(ndb.at[band], got.at[band], local_sem)
    own_pixels.start()
    copies = []
    for i, other in enumerate(others):
        copies.append(pltpu.make_async_remote_copy(
            src_ref=ndb.at[other], dst_ref=got.at[band], send_sem=pix_send.at[i], recv_sem=pix_recv.at[i],
            device_id=(sky, other), device_id_type=MESH,
        ))
        copies[-1].start()
    own_pixels.wait()
    for copy in copies:
        copy.wait_recv()
    for t in range(4):
        val = got[t].astype(F32)
        for half in range(2):
            wide[half, t * BPD * RPD:(t + 1) * BPD * RPD, :] = val[:, half * 128:half * 128 + 128]
    pixels = [[wide[half, pl.ds(r, BANDS, stride=RPD), :] for half in range(2)] for r in range(RPD)]
    gram = jnp.zeros((BANDS, 128), F32)
    for d in range(4):
        x = jnp.concatenate([v for r in range(DOM) for v in pixels[d * DOM + r]], axis=1).astype(BF)
        x = jnp.concatenate([x, jnp.zeros((128 - BANDS, x.shape[1]), BF)], axis=0)
        block = mm(x[:BANDS], x, NT)
        gram = gram + (pltpu.roll(block, 32 * d, 1) if d else block)
    part[...] = gram
    for i, other in enumerate(others):
        copies.append(pltpu.make_async_remote_copy(
            src_ref=part, dst_ref=parts.at[i], send_sem=cov_send.at[i], recv_sem=cov_recv.at[i],
            device_id=(sky, other), device_id_type=MESH,
        ))
        copies[-1].start()
    for copy in copies[3:]:
        copy.wait_recv()
    total = (gram + parts[1]) + (parts[0] + parts[2])
    row = lax.broadcasted_iota(jnp.int32, (BANDS, 128), 0)
    col = lax.broadcasted_iota(jnp.int32, (BANDS, 128), 1)
    systems = []
    for d in range(4):
        count = length_of[d * DOM] + length_of[d * DOM + 1] + length_of[d * DOM + 2] + length_of[d * DOM + 3]
        cov = pltpu.roll(total, 128 - 32 * d, 1) if d else total
        cov = cov / jnp.full((1, 128), count, jnp.int32).astype(F32)
        diagonal = jnp.where(row == col, cov, 0.0)
        trace = jnp.sum(jnp.sum(diagonal, axis=1, keepdims=True), axis=0, keepdims=True)
        work = jnp.where(col < BANDS, cov, 0.0) + jnp.where(row == col, (RIDGE / BANDS) * trace, 0.0)
        systems.append(jnp.where(col == BANDS, 1.0, work))
    for j in range(BANDS):
        for d in range(4):
            work = systems[d]
            pivot = work[j:j + 1, :] / work[j:j + 1, j:j + 1]
            systems[d] = jnp.where(row == j, pivot, work - work[:, j:j + 1] * pivot)
    for d in range(4):
        solved = systems[d][:, BANDS:BANDS + 1]
        weights = solved / jnp.sum(solved, axis=0, keepdims=True)
        for r in range(DOM):
            at = d * DOM + r
            clean = [jnp.sum(weights * v, axis=0, keepdims=True) for v in pixels[at]]
            out_ref[at:at + 1, :] = jnp.concatenate(clean, axis=1)
    out_copies.wait_send()
    back_copies.wait_send()
    for copy in copies:
        copy.wait_send()


def on_device(band_maps, cycle_weight, cycle_len, m_order, legendre, band_start):
    whole = pl.BlockSpec(memory_space=pl.ANY)
    vmem = pltpu.VMEM
    dma = pltpu.SemaphoreType.DMA
    return pl.pallas_call(
        whole_kernel,
        out_shape=jax.ShapeDtypeStruct((RPD, QUARTER), F32),
        in_specs=[whole] * 7,
        out_specs=pl.BlockSpec(memory_space=vmem),
        scratch_shapes=[
            vmem((BPD * RPD, 4 * QUARTER), F32),
            pltpu.SMEM((RPD,), F32),
            pltpu.SMEM((RPD,), jnp.int32),
            pltpu.SMEM((M,), jnp.int32),
            vmem((8, 128), jnp.int32),
            pltpu.SMEM((1,), jnp.int32),
            vmem((SLOTS, LB, 512), BF),
            vmem((11, BPD * RPD, 128), F32),
            vmem((11, BPD * RPD, 128), F32),
            vmem((M, 128), F32),
            vmem((RPD, 64, QUARTER), F32),
            vmem((RPD, 32, 2 * QUARTER), BF),
            vmem((RPD, 32, 2 * QUARTER), BF),
            vmem((M, M), BF),
            vmem((NDEV, SLOTS, 128), BF),
            vmem((NDEV, SLOTS, 128), BF),
            vmem((4, 4 * GROUPS * SLOTS, 128), F32),
            vmem((4, 4 * GROUPS * SLOTS, 128), F32),
            vmem((NDEV, SLOTS, 128), BACK),
            vmem((NDEV, SLOTS, 128), BACK),
            vmem((4, RPD, BPD, QUARTER), F32),
            vmem((3, 20, BPD, 128), F32),
            vmem((8, BPD * RPD, 128), F32),
            vmem((4, BPD * RPD, QUARTER), BF),
            vmem((4, BPD * RPD, QUARTER), BF),
            vmem((2, 4 * BPD * RPD, 128), F32),
            vmem((BANDS, 128), F32),
            vmem((3, BANDS, 128), F32),
            dma((6,)),
            dma((SLOTS,)),
            dma,
            dma((2,)),
            dma((2,)),
            dma((3,)),
            dma((3,)),
            dma((3,)),
            dma((3,)),
        ],
        compiler_params=pltpu.CompilerParams(
            collective_id=0, has_side_effects=True, vmem_limit_bytes=56 << 20
        ),
        name="needlet_ilc",
    )(
        band_maps.reshape(BPD * RPD, 4 * QUARTER), cycle_weight, cycle_len, m_order, m_order.reshape(8, 128),
        legendre, band_start,
    )


def solution(mesh):
    placed = (P("band", "sky", None), P("sky"), P("sky"), P(), P(("sky", "band"), None, None), P())
    return jax.shard_map(
        on_device, mesh=mesh, in_specs=placed, out_specs=P("sky", "band"), check_vma=False
    )
```

profile of v0, /device:TPU:0, one launch (start us, length us, event | category | flops | bytes accessed | tf_op | source)
XLA Modules:
  0.0 54.3 jit_solution(8584681416328581441)
XLA Ops:
  0.7 52.3 %needlet_ilc.1 = f32[16,256]{1,0:T(8,128)} custom-call(f32[64,1024]{1,0:T(8,128)} %bitcast.2, f32[16]{0:T(128)} %weight_hbm.1, s32[16]{0:T(128)} %len_hbm.1, s32[1024]{0:T(1024)} %order_hbm.1, s32[8,128]{1,0:T(8,128)} %bitcast.3, bf16[8,1024,512]{2,1,0:T(8,128)(2,1)} %leg_hbm.1, s32[1]{0:T(128)S(6)} %copy.8.start_hbm), custom_call_target="tpu_custom_call" | custom-call | tf_op jit(solution)/shard_map/needlet_ilc/pallas_call | solution.py:444
  52.9 1.3 %copy.9 = f32[16,256]{1,0:T(8,128)} copy(f32[16,256]{1,0:T(8,128)} %needlet_ilc.1) | data formatting | bytes 32768
where the time goes:
time: 54.5 us; the launch traced here: 54.3 us
  Pallas kernels  52.3 us (96%)
  local copies, waits for them, and re-layouts  1.32 us (2%)
  between operations  0.66 us (1%)
    pallas_call x1, Pallas kernels, on_device(): pl.pallas_call(whole_kernel, out_shape=jax.ShapeDtypeStruct((RPD, QUARTER...  52.3 us
    unnamed x1, local copies, waits for them, and re-layouts  1.32 us

commit v1 on v0

--- a/solution.py
+++ b/solution.py
@@ -93,9 +93,10 @@
 
 
 def whole_kernel(
-    maps_hbm, weight_hbm, len_hbm, order_hbm, order_rows_hbm, leg_hbm, start_hbm, out_ref,
+    maps_hbm, weight_hbm, len_hbm, order_hbm, order_rows_hbm, leg_hbm, start_hbm, low_ref, high_ref,
     maps, weight, length_of, order, order_vec, start, leg,
-    xs, xr, cs, tp, th, tl, hot, msg, arrived, hx, hy, back, returned, nq, pb, nd, ndb, got, wide, part, parts,
+    xs, xr, cs, tp, th, tl, hot, flat_ref, msg, arrived, hx, hy, filtered, back, returned, pb, ndb, got, wide,
+    part, parts,
     small_sem, leg_sem, local_sem, send_sem, recv_sem, pix_send, pix_recv, cov_send, cov_recv,
 ):
     sky = lax.axis_index("sky")
@@ -119,14 +120,64 @@
 
     barrier = pltpu.get_barrier_semaphore()
 
-    def greet(i):
-        row = lax.rem(sky + i, 32)
-        for column in bands:
-            pl.semaphore_signal(barrier, inc=1, device_id=(row, column), device_id_type=MESH)
-
-    for column in others:
-        pl.semaphore_signal(barrier, inc=1, device_id=(sky, column), device_id_type=MESH)
-    greet(1)
+    def signal(row, column):
+        pl.semaphore_signal(barrier, inc=1, device_id=(row, column), device_id_type=MESH)
+
+    node = lax.rem(sky, 8)
+    branch = sky // 8
+    leader = band == 0
+    inner_leader = leader & (node != 0)
+    branch_leader = leader & (node == 0) & (branch != 0)
+    root = leader & (sky == 0)
+
+    def leaders_below():
+        for i in range(1, 8):
+            signal(branch * 8 + i, 0)
+
+    def bands_below():
+        for i in range(1, 4):
+            signal(sky, i)
+
+    def enter(step):
+        if step == 0:
+            @pl.when(band != 0)
+            def _():
+                signal(sky, 0)
+        if step == 1:
+            @pl.when(inner_leader)
+            def _():
+                pl.semaphore_wait(barrier, 3)
+                signal(branch * 8, 0)
+        if step == 2:
+            @pl.when(branch_leader)
+            def _():
+                pl.semaphore_wait(barrier, 10)
+                signal(0, 0)
+        if step == 3:
+            @pl.when(root)
+            def _():
+                pl.semaphore_wait(barrier, 13)
+                for i in range(1, 4):
+                    signal(8 * i, 0)
+                leaders_below()
+                bands_below()
+        if step == 4:
+            @pl.when(branch_leader)
+            def _():
+                pl.semaphore_wait(barrier, 1)
+                leaders_below()
+                bands_below()
+        if step == 5:
+            @pl.when(inner_leader)
+            def _():
+                pl.semaphore_wait(barrier, 1)
+                bands_below()
+        if step == 6:
+            @pl.when(band != 0)
+            def _():
+                pl.semaphore_wait(barrier, 1)
+
+    enter(0)
 
     flip = reversal()
     for copy in small:
@@ -140,6 +191,7 @@
         turned = mm(maps[:, block * QUARTER:(block + 1) * QUARTER], flip, NN, lax.Precision.HIGHEST)
         xr[6 - 2 * block] = turned[:, 0:128]
         xr[7 - 2 * block] = turned[:, 128:256]
+    enter(1)
     inner, outer = order_rows()
     lane4 = lax.broadcasted_iota(jnp.int32, (BPD, 128), 1)
     pixel = lax.broadcasted_iota(jnp.int32, (BPD, QUARTER), 1)
@@ -209,9 +261,10 @@
     def analyse_four(i, carry):
         for j in range(4):
             analyse(4 * i + j, carry)
+        for step in range(4):
+            pl.when(i == step)(functools.partial(enter, step + 2))
         return carry
 
-    lax.fori_loop(2, 32, lambda i, carry: (greet(i), carry)[1], 0)
     lax.fori_loop(0, RPD // 4, analyse_four, 0)
 
     flat = jnp.concatenate([cs[pl.ds(a, 128, stride=8), :].astype(BF) for a in range(8)], axis=1)
@@ -220,40 +273,50 @@
     lane128 = lax.broadcasted_iota(jnp.int32, (128, 128), 1).astype(F32)
     for block in range(8):
         target = jnp.broadcast_to(where_to[block:block + 1], (128, 128)).T
-        row_hot = jnp.concatenate(
+        hot[block * 128:block * 128 + 128, :] = jnp.concatenate(
             [jnp.where(target == lane128 + 128.0 * a, 1.0, 0.0).astype(BF) for a in range(8)], axis=1
         )
-        hot[block * 128:block * 128 + 128, :] = row_hot
-        moved = mm(row_hot, flat, NT)
-        msg[block * 16:block * 16 + 16] = moved.reshape(16, SLOTS, 128).astype(BF)
-
-    own = pltpu.make_async_copy(msg.at[me], arrived.at[me], local_sem)
-    own.start()
-    pl.semaphore_wait(barrier, NDEV - 1)
-
-    def everyone(src, dst, phase):
-        def one(row, column):
-            pltpu.make_async_remote_copy(
-                src_ref=src.at[row * 4 + column], dst_ref=dst.at[me], send_sem=send_sem.at[phase],
-                recv_sem=recv_sem.at[phase], device_id=(row, column), device_id_type=MESH,
-            ).start()
-
-        for column in others:
-            one(sky, column)
-
-        def rows(i, carry):
-            row = lax.rem(sky + i, 32)
-            for column in bands:
-                one(row, column)
-            return carry
-
-        lax.fori_loop(1, 32, rows, 0)
+
+    def send(src, dst, phase, row, column):
+        pltpu.make_async_remote_copy(
+            src_ref=src.at[row * 4 + column], dst_ref=dst.at[me], send_sem=send_sem.at[phase],
+            recv_sem=recv_sem.at[phase], device_id=(row, column), device_id_type=MESH,
+        ).start()
+
+    def sent(src, dst, phase):
         return pltpu.make_async_remote_copy(
             src_ref=src.at[pl.ds(0, NDEV - 1)], dst_ref=dst.at[pl.ds(0, NDEV - 1)], send_sem=send_sem.at[phase],
             recv_sem=recv_sem.at[phase], device_id=(sky, others[0]), device_id_type=MESH,
         )
 
-    out_copies = everyone(msg, arrived, 0)
+    def send_rows(src, dst, phase, base, count, here):
+        def rows(i, carry):
+            row = base + lax.rem(here + i, count)
+            for column in bands:
+                send(src, dst, phase, row, column)
+            return carry
+
+        lax.fori_loop(1, count, rows, 0)
+        twin = base + here
+        for column in others:
+            send(src, dst, phase, twin, column)
+        pl.when(twin != sky)(lambda: send(src, dst, phase, twin, band))
+
+    enter(6)
+
+    def slot_block(i, carry):
+        block = lax.rem(sky // 4 + i, 8)
+        at = pl.multiple_of(block * 128, 128)
+        moved = mm(hot[pl.ds(at, 128), :], flat_ref[...], NT)
+        msg[pl.ds(pl.multiple_of(block * 16, 16), 16)] = moved.reshape(16, SLOTS, 128).astype(BF)
+        send_rows(msg, arrived, 0, block * 4, 4, lax.rem(sky, 4))
+        return carry
+
+    flat_ref[...] = flat
+    lax.fori_loop(0, 8, slot_block, 0)
+    own = pltpu.make_async_copy(msg.at[me], arrived.at[me], local_sem)
+    own.start()
+    out_copies = sent(msg, arrived, 0)
     window_at = lax.broadcasted_iota(jnp.int32, (8, LB), 1).astype(F32)
     taper = window_taper(window_at)[0:1] * (1.0 / math.sqrt(LB))
     degree = lax.broadcasted_iota(jnp.int32, (1, LB), 1) + start[0]
@@ -273,27 +336,35 @@
             [hx[tile, pl.ds(m, 4 * GROUPS, stride=8), :].astype(BF) for tile in range(4)], axis=1
         )
         loads[m].wait()
-        table = leg[m]
-        harmonic = mm(coeff, table, NT)
-        result = mm((harmonic * keep).astype(BF), table, NN)
-        for tile in range(4):
-            hy[tile, pl.ds(m, 4 * GROUPS, stride=8), :] = result[:, tile * 128:tile * 128 + 128]
-    for tile in range(4):
-        for source in range(4):
-            done = []
-            for g in range(GROUPS):
-                at = (source * GROUPS + g) * 8
-                done.append(hy[tile, at:at + 8, :])
-            for i, val in enumerate(swap_blocks(done, lane_group)):
-                back[(tile * 8 + i) * 4 + source] = val.astype(back.dtype)
-
+        filtered[m] = (mm(coeff, leg[m], NT) * keep).astype(BF)
+
+    def cycle_half(i, carry):
+        half = lax.rem(sky + i, 2)
+        at = pl.multiple_of(half * QUARTER, QUARTER)
+        for m in range(SLOTS):
+            result = mm(filtered[m], leg[m, :, pl.ds(at, QUARTER)], NN)
+            for side in range(2):
+                hy[side, pl.ds(m, 4 * GROUPS, stride=8), :] = result[:, side * 128:side * 128 + 128]
+        for side in range(2):
+            for source in range(4):
+                done = []
+                for g in range(GROUPS):
+                    row = (source * GROUPS + g) * 8
+                    done.append(hy[side, row:row + 8, :])
+                for k, val in enumerate(swap_blocks(done, lane_group)):
+                    back[(half * 16 + side * 8 + k) * 4 + source] = val.astype(back.dtype)
+        send_rows(back, returned, 1, half * 16, 16, lax.rem(sky, 16))
+        return carry
+
+    lax.fori_loop(0, 2, cycle_half, 0)
     own_back = pltpu.make_async_copy(back.at[me], returned.at[me], local_sem)
     own_back.start()
-    back_copies = everyone(back, returned, 1)
-    for i in range(3):
-        for tile in range(20):
-            if tile not in (8, 9, 10):
-                pb[i, tile] = jnp.zeros((BPD, 128), F32)
+    back_copies = sent(back, returned, 1)
+    for k in range(4):
+        for i in range(3):
+            for tile in range(20):
+                if tile not in (8, 9, 10):
+                    pb[k, i, tile] = jnp.zeros((BPD, 128), F32)
     flip16 = flip.astype(BF)
     own_back.wait()
     back_copies.wait_recv()
@@ -313,7 +384,7 @@
                 val = jnp.where(lane1 == 0, 0.5 * val, val)
             cs[pl.ds(a, 128, stride=8), :] = val
 
-    def synthesise(r, carry):
+    def cycle(r):
         cos_p = tp[r, 0:32, :]
         sin_p = tp[r, 32:64, :]
         table_hi = jnp.concatenate([th[r]] * 4, axis=0)
@@ -339,85 +410,87 @@
             for i, total in enumerate((ce + co - de - do, ce - co + de - do, ce - co - de + do, ce + co + de + do)):
                 quarters[i].append(jnp.sum(total, axis=0, keepdims=True))
         inside = pixel < length_of[r] // 4
-        for i in range(4):
-            val = jnp.where(inside, jnp.concatenate(quarters[i], axis=0), 0.0)
-            nq[i, r] = val.astype(BF).astype(F32)
+        return [jnp.where(inside, jnp.concatenate(q, axis=0), 0.0).astype(BF).astype(F32) for q in quarters]
+
+    def pixel_copy(d, i):
+        return pltpu.make_async_remote_copy(
+            src_ref=ndb.at[d, others[i]], dst_ref=got.at[d, band], send_sem=pix_send.at[d, i],
+            recv_sem=pix_recv.at[d, i], device_id=(sky, others[i]), device_id_type=MESH,
+        )
+
+    def gram_copy(d, i):
+        return pltpu.make_async_remote_copy(
+            src_ref=part.at[d], dst_ref=parts.at[d, i], send_sem=cov_send.at[d, i], recv_sem=cov_recv.at[d, i],
+            device_id=(sky, others[i]), device_id_type=MESH,
+        )
+
+    def pixels_of(d):
+        cycles = [cycle(d * DOM + k) for k in range(DOM)]
+        turned = mm(
+            jnp.concatenate([q[i] for i in (1, 3) for q in cycles], axis=0).astype(BF), flip16, NN
+        )
+        columns = [[] for _ in range(8)]
+        for k in range(DOM):
+            length = length_of[d * DOM + k]
+            tiles = []
+            vals = (turned[k * 4:k * 4 + 4], cycles[k][2], turned[16 + k * 4:16 + k * 4 + 4])
+            for i, offset in enumerate((length // 2 - QUARTER, length // 2, length - QUARTER)):
+                tile = (offset + 1024) // 128 - 8
+                rest = offset - tile * 128
+                low = pltpu.roll(vals[i][:, :128], rest, 1)
+                high = pltpu.roll(vals[i][:, 128:], rest, 1)
+                wrapped = lane4 < rest
+                pb[k, i, 8] = jnp.where(wrapped, 0.0, low)
+                pb[k, i, 9] = jnp.where(wrapped, low, high)
+                pb[k, i, 10] = jnp.where(wrapped, high, 0.0)
+                tiles.append(tile)
+            for t in range(8):
+                total = pb[k, 0, 8 + t - tiles[0]] + pb[k, 1, 8 + t - tiles[1]] + pb[k, 2, 8 + t - tiles[2]]
+                if t < 2:
+                    total = total + cycles[k][0][:, t * 128:t * 128 + 128]
+                columns[t].append(total)
+        for t in range(4):
+            ndb[d, t] = jnp.concatenate(
+                [jnp.concatenate(columns[2 * t + half], axis=0) for half in range(2)], axis=1
+            ).astype(BF)
+        for i in range(3):
+            pixel_copy(d, i).start()
+        got[d, band] = ndb[d, band]
+
+    def gram_of(d):
+        for i in range(3):
+            pixel_copy(d, i).wait_recv()
+        for t in range(4):
+            val = got[d, t].astype(F32)
+            for k in range(DOM):
+                for half in range(2):
+                    wide[d, k, half, 4 * t:4 * t + 4, :] = val[4 * k:4 * k + 4, half * 128:half * 128 + 128]
+        x = jnp.concatenate([wide[d, k, half] for k in range(DOM) for half in range(2)], axis=1).astype(BF)
+        tall = jnp.concatenate([x, jnp.zeros((128 - BANDS, x.shape[1]), BF)], axis=0)
+        part[d] = mm(x, tall, NT)
+        for i in range(3):
+            gram_copy(d, i).start()
+
+    def domain(d, carry):
+        pixels_of(d)
+        pl.when(d > 0)(lambda: gram_of(d - 1))
         return carry
 
-    lax.fori_loop(0, RPD, synthesise, 0, unroll=4)
-    for i in (1, 3):
-        whole = nq[i].reshape(RPD * BPD, QUARTER).astype(BF)
-        nq[i] = mm(whole, flip16, NN).reshape(RPD, BPD, QUARTER)
-
-    def place(r, carry):
-        length = length_of[r]
-        tiles = []
-        for i, offset in ((1, length // 2 - QUARTER), (2, length // 2), (3, length - QUARTER)):
-            tile = (offset + 1024) // 128 - 8
-            rest = offset - tile * 128
-            val = nq[i, r]
-            low = pltpu.roll(val[:, :128], rest, 1)
-            high = pltpu.roll(val[:, 128:], rest, 1)
-            wrapped = lane4 < rest
-            pb[i - 1, 8] = jnp.where(wrapped, 0.0, low)
-            pb[i - 1, 9] = jnp.where(wrapped, low, high)
-            pb[i - 1, 10] = jnp.where(wrapped, high, 0.0)
-            tiles.append(tile)
-        first = nq[0, r]
-        for t in range(8):
-            total = pb[0, 8 + t - tiles[0]] + pb[1, 8 + t - tiles[1]] + pb[2, 8 + t - tiles[2]]
-            if t < 2:
-                total = total + first[:, t * 128:t * 128 + 128]
-            nd[t, pl.ds(r, BPD, stride=RPD), :] = total
-        return carry
-
-    lax.fori_loop(0, RPD, place, 0, unroll=2)
-    for t in range(4):
-        ndb[t] = jnp.concatenate([nd[2 * t], nd[2 * t + 1]], axis=1).astype(BF)
-
-    own_pixels = pltpu.make_async_copy(ndb.at[band], got.at[band], local_sem)
-    own_pixels.start()
-    copies = []
-    for i, other in enumerate(others):
-        copies.append(pltpu.make_async_remote_copy(
-            src_ref=ndb.at[other], dst_ref=got.at[band], send_sem=pix_send.at[i], recv_sem=pix_recv.at[i],
-            device_id=(sky, other), device_id_type=MESH,
-        ))
-        copies[-1].start()
-    own_pixels.wait()
-    for copy in copies:
-        copy.wait_recv()
-    for t in range(4):
-        val = got[t].astype(F32)
-        for half in range(2):
-            wide[half, t * BPD * RPD:(t + 1) * BPD * RPD, :] = val[:, half * 128:half * 128 + 128]
-    pixels = [[wide[half, pl.ds(r, BANDS, stride=RPD), :] for half in range(2)] for r in range(RPD)]
-    gram = jnp.zeros((BANDS, 128), F32)
-    for d in range(4):
-        x = jnp.concatenate([v for r in range(DOM) for v in pixels[d * DOM + r]], axis=1).astype(BF)
-        x = jnp.concatenate([x, jnp.zeros((128 - BANDS, x.shape[1]), BF)], axis=0)
-        block = mm(x[:BANDS], x, NT)
-        gram = gram + (pltpu.roll(block, 32 * d, 1) if d else block)
-    part[...] = gram
-    for i, other in enumerate(others):
-        copies.append(pltpu.make_async_remote_copy(
-            src_ref=part, dst_ref=parts.at[i], send_sem=cov_send.at[i], recv_sem=cov_recv.at[i],
-            device_id=(sky, other), device_id_type=MESH,
-        ))
-        copies[-1].start()
-    for copy in copies[3:]:
-        copy.wait_recv()
-    total = (gram + parts[1]) + (parts[0] + parts[2])
+    lax.fori_loop(0, 4, domain, 0)
+
+    gram_of(3)
     row = lax.broadcasted_iota(jnp.int32, (BANDS, 128), 0)
     col = lax.broadcasted_iota(jnp.int32, (BANDS, 128), 1)
     systems = []
     for d in range(4):
+        for i in range(3):
+            gram_copy(d, i).wait_recv()
         count = length_of[d * DOM] + length_of[d * DOM + 1] + length_of[d * DOM + 2] + length_of[d * DOM + 3]
-        cov = pltpu.roll(total, 128 - 32 * d, 1) if d else total
+        cov = (part[d] + parts[d, 1]) + (parts[d, 0] + parts[d, 2])
         cov = cov / jnp.full((1, 128), count, jnp.int32).astype(F32)
         diagonal = jnp.where(row == col, cov, 0.0)
         trace = jnp.sum(jnp.sum(diagonal, axis=1, keepdims=True), axis=0, keepdims=True)
-        work = jnp.where(col < BANDS, cov, 0.0) + jnp.where(row == col, (RIDGE / BANDS) * trace, 0.0)
+        work = cov + jnp.where(row == col, (RIDGE / BANDS) * trace, 0.0)
         systems.append(jnp.where(col == BANDS, 1.0, work))
     for j in range(BANDS):
         for d in range(4):
@@ -427,25 +500,30 @@
     for d in range(4):
         solved = systems[d][:, BANDS:BANDS + 1]
         weights = solved / jnp.sum(solved, axis=0, keepdims=True)
-        for r in range(DOM):
-            at = d * DOM + r
-            clean = [jnp.sum(weights * v, axis=0, keepdims=True) for v in pixels[at]]
-            out_ref[at:at + 1, :] = jnp.concatenate(clean, axis=1)
+        for k in range(DOM):
+            at = d * DOM + k
+            terms = [weights * wide[d, k, half] for half in range(2)]
+            for ref, first in ((low_ref, 0), (high_ref, 8)):
+                ref[at:at + 1, :] = jnp.concatenate(
+                    [jnp.sum(v[first:first + 8], axis=0, keepdims=True) for v in terms], axis=1
+                )
     out_copies.wait_send()
     back_copies.wait_send()
-    for copy in copies:
-        copy.wait_send()
+    for d in range(4):
+        for i in range(3):
+            pixel_copy(d, i).wait_send()
+            gram_copy(d, i).wait_send()
 
 
 def on_device(band_maps, cycle_weight, cycle_len, m_order, legendre, band_start):
     whole = pl.BlockSpec(memory_space=pl.ANY)
     vmem = pltpu.VMEM
     dma = pltpu.SemaphoreType.DMA
-    return pl.pallas_call(
+    low, high = pl.pallas_call(
         whole_kernel,
-        out_shape=jax.ShapeDtypeStruct((RPD, QUARTER), F32),
+        out_shape=[jax.ShapeDtypeStruct((RPD, QUARTER), F32)] * 2,
         in_specs=[whole] * 7,
-        out_specs=pl.BlockSpec(memory_space=vmem),
+        out_specs=[pl.BlockSpec(memory_space=vmem)] * 2,
         scratch_shapes=[
             vmem((BPD * RPD, 4 * QUARTER), F32),
             pltpu.SMEM((RPD,), F32),
@@ -461,29 +539,29 @@
             vmem((RPD, 32, 2 * QUARTER), BF),
             vmem((RPD, 32, 2 * QUARTER), BF),
             vmem((M, M), BF),
+            vmem((128, M), BF),
             vmem((NDEV, SLOTS, 128), BF),
             vmem((NDEV, SLOTS, 128), BF),
             vmem((4, 4 * GROUPS * SLOTS, 128), F32),
-            vmem((4, 4 * GROUPS * SLOTS, 128), F32),
+            vmem((2, 4 * GROUPS * SLOTS, 128), F32),
+            vmem((SLOTS, 4 * GROUPS, LB), BF),
             vmem((NDEV, SLOTS, 128), BACK),
             vmem((NDEV, SLOTS, 128), BACK),
-            vmem((4, RPD, BPD, QUARTER), F32),
-            vmem((3, 20, BPD, 128), F32),
-            vmem((8, BPD * RPD, 128), F32),
-            vmem((4, BPD * RPD, QUARTER), BF),
-            vmem((4, BPD * RPD, QUARTER), BF),
-            vmem((2, 4 * BPD * RPD, 128), F32),
-            vmem((BANDS, 128), F32),
-            vmem((3, BANDS, 128), F32),
+            vmem((DOM, 3, 20, BPD, 128), F32),
+            vmem((4, 4, 4 * DOM, QUARTER), BF),
+            vmem((4, 4, 4 * DOM, QUARTER), BF),
+            vmem((4, DOM, 2, BANDS, 128), F32),
+            vmem((4, BANDS, 128), F32),
+            vmem((4, 3, BANDS, 128), F32),
             dma((6,)),
             dma((SLOTS,)),
             dma,
             dma((2,)),
             dma((2,)),
-            dma((3,)),
-            dma((3,)),
-            dma((3,)),
-            dma((3,)),
+            dma((4, 3)),
+            dma((4, 3)),
+            dma((4, 3)),
+            dma((4, 3)),
         ],
         compiler_params=pltpu.CompilerParams(
             collective_id=0, has_side_effects=True, vmem_limit_bytes=56 << 20
@@ -493,6 +571,7 @@
         band_maps.reshape(BPD * RPD, 4 * QUARTER), cycle_weight, cycle_len, m_order, m_order.reshape(8, 128),
         legendre, band_start,
     )
+    return low + high
 
 
 def solution(mesh):

time: 54.5 us -> 57.1 us (1.048)
  Pallas kernels: 52.3 us -> 54.9 us
  other arithmetic: 0 us -> 1.34 us
  local copies, waits for them, and re-layouts: 1.32 us -> 0 us
    pallas_call x1, Pallas kernels: 52.3 us -> 54.9 us  [on_device(): pl.pallas_call(whole_kernel, out_shape=[jax.ShapeDtypeStruct((RPD, QUARTE...]
    add x0 -> x1, other arithmetic: none -> 1.34 us  [on_device(): return low + high]
    unnamed x1 -> x0, local copies, waits for them, and re-layouts: 1.32 us -> none
where the time goes in v1:
time: 57.1 us; the launch traced here: 56.9 us
  Pallas kernels  54.9 us (96%)
  other arithmetic  1.34 us (2%)
  between operations  0.66 us (1%)
    pallas_call x1, Pallas kernels, on_device(): pl.pallas_call(whole_kernel, out_shape=[jax.ShapeDtypeStruct((RPD, QUARTE...  54.9 us
    add x1, other arithmetic, on_device(): return low + high  1.34 us

profile of v1, /device:TPU:0, one launch (start us, length us, event | category | flops | bytes accessed | tf_op | source)
XLA Modules:
  0.0 56.9 jit_solution(6858867284466589169)
XLA Ops:
  0.7 54.9 %needlet_ilc.1 = (f32[16,256]{1,0:T(8,128)}, f32[16,256]{1,0:T(8,128)}) custom-call(f32[64,1024]{1,0:T(8,128)} %bitcast.2, f32[16]{0:T(128)} %weight_hbm.1, s32[16]{0:T(128)} %len_hbm.1, s32[1024]{0:T(1024)} %order_hbm.1, s32[8,128]{1,0:T(8,128)} %bitcast.3, bf16[8,1024,512]{2,1,0:T(8,128)(2,1)} %leg_hbm.1, s32[1]{0:T(128)S(6)} %copy.7.start_hbm), custom_call_target="tpu_custom_call" | custom-call | tf_op jit(solution)/shard_map/needlet_ilc/pallas_call | solution.py:522
  55.5 1.3 %add.3 = f32[16,256]{1,0:T(8,128)} add(f32[16,256]{1,0:T(8,128)} %get-tuple-element.7, f32[16,256]{1,0:T(8,128)} %get-tuple-element.8) | non-fusion elementwise | flops 4096 | bytes 49152 | tf_op jit(solution)/shard_map/add | solution.py:574

commit v2 on v0

--- a/solution.py
+++ b/solution.py
@@ -22,7 +22,7 @@
 MESH = pl.DeviceIdType.MESH
 BF = jnp.bfloat16
 F32 = jnp.float32
-BACK = jnp.float32
+BACK = jnp.bfloat16
 NT = (((1,), (1,)), ((), ()))
 NN = (((1,), (0,)), ((), ()))
 
@@ -301,11 +301,11 @@
     turned = jnp.concatenate(
         [returned[d * 16:d * 16 + 16].astype(F32).reshape(128, 128).T for d in range(8)], axis=1
     )
-    stacked = jnp.concatenate(split(turned), axis=0)
+    stacked = turned.astype(BF)
     lane1 = lax.broadcasted_iota(jnp.int32, (128, 128), 1)
     for pair in range(4):
         moved = mm(stacked, hot[:, pair * QUARTER:(pair + 1) * QUARTER], NN)
-        natural = (moved[0:128] + moved[128:256]) * (2.0 / math.sqrt(M))
+        natural = moved
         for half in range(2):
             a = pair * 2 + half
             val = natural[:, half * 128:half * 128 + 128]
@@ -324,10 +324,8 @@
             v = cs[pl.ds(at, 8), :]
             for c in range(4):
                 pieces.append(jnp.where(quad_group == c, v, 0.0))
-        hi, lo = split(jnp.concatenate(pieces, axis=0))
-        full = mm(jnp.concatenate([hi, lo], axis=1), jnp.concatenate([table_hi, table_hi], axis=0), NN) + mm(
-            hi, table_lo, NN
-        )
+        hi = jnp.concatenate(pieces, axis=0).astype(BF)
+        full = mm(jnp.concatenate([hi, hi], axis=1), jnp.concatenate([table_hi, table_lo], axis=0), NN)
         quarters = [[], [], [], []]
         for b in range(BPD):
             re = full[(2 * b) * 32:(2 * b) * 32 + 32]
@@ -340,7 +338,7 @@
                 quarters[i].append(jnp.sum(total, axis=0, keepdims=True))
         inside = pixel < length_of[r] // 4
         for i in range(4):
-            val = jnp.where(inside, jnp.concatenate(quarters[i], axis=0), 0.0)
+            val = jnp.where(inside, jnp.concatenate(quarters[i], axis=0) * (2.0 / math.sqrt(M)), 0.0)
             nq[i, r] = val.astype(BF).astype(F32)
         return carry
 

time: 54.5 us -> 50.3 us (0.923)
  Pallas kernels: 52.3 us -> 48.2 us
    pallas_call x1, Pallas kernels: 52.3 us -> 48.2 us  [on_device(): pl.pallas_call(whole_kernel, out_shape=jax.ShapeDtypeStruct((RPD, QUARTER...]
where the time goes in v2:
time: 50.3 us; the launch traced here: 50.2 us
  Pallas kernels  48.2 us (96%)
  local copies, waits for them, and re-layouts  1.32 us (3%)
  between operations  0.66 us (1%)
    pallas_call x1, Pallas kernels, on_device(): pl.pallas_call(whole_kernel, out_shape=jax.ShapeDtypeStruct((RPD, QUARTER...  48.2 us
    unnamed x1, local copies, waits for them, and re-layouts  1.32 us

profile of v2, /device:TPU:0, one launch (start us, length us, event | category | flops | bytes accessed | tf_op | source)
XLA Modules:
  0.0 50.2 jit_solution(3897225385278118606)
XLA Ops:
  0.7 48.2 %needlet_ilc.1 = f32[16,256]{1,0:T(8,128)} custom-call(f32[64,1024]{1,0:T(8,128)} %bitcast.2, f32[16]{0:T(128)} %weight_hbm.1, s32[16]{0:T(128)} %len_hbm.1, s32[1024]{0:T(1024)} %order_hbm.1, s32[8,128]{1,0:T(8,128)} %bitcast.3, bf16[8,1024,512]{2,1,0:T(8,128)(2,1)} %leg_hbm.1, s32[1]{0:T(128)S(6)} %copy.8.start_hbm), custom_call_target="tpu_custom_call" | custom-call | tf_op jit(solution)/shard_map/needlet_ilc/pallas_call | solution.py:442
  48.8 1.3 %copy.9 = f32[16,256]{1,0:T(8,128)} copy(f32[16,256]{1,0:T(8,128)} %needlet_ilc.1) | data formatting | bytes 32768

commit v3 on v1

--- a/solution.py
+++ b/solution.py
@@ -22,7 +22,7 @@
 MESH = pl.DeviceIdType.MESH
 BF = jnp.bfloat16
 F32 = jnp.float32
-BACK = jnp.float32
+BACK = jnp.bfloat16
 NT = (((1,), (1,)), ((), ()))
 NN = (((1,), (0,)), ((), ()))
 
@@ -93,7 +93,7 @@
 
 
 def whole_kernel(
-    maps_hbm, weight_hbm, len_hbm, order_hbm, order_rows_hbm, leg_hbm, start_hbm, low_ref, high_ref,
+    maps_hbm, weight_hbm, len_hbm, order_hbm, order_rows_hbm, leg_hbm, start_hbm, out_ref,
     maps, weight, length_of, order, order_vec, start, leg,
     xs, xr, cs, tp, th, tl, hot, flat_ref, msg, arrived, hx, hy, filtered, back, returned, pb, ndb, got, wide,
     part, parts,
@@ -120,64 +120,15 @@
 
     barrier = pltpu.get_barrier_semaphore()
 
-    def signal(row, column):
-        pl.semaphore_signal(barrier, inc=1, device_id=(row, column), device_id_type=MESH)
-
-    node = lax.rem(sky, 8)
-    branch = sky // 8
-    leader = band == 0
-    inner_leader = leader & (node != 0)
-    branch_leader = leader & (node == 0) & (branch != 0)
-    root = leader & (sky == 0)
-
-    def leaders_below():
-        for i in range(1, 8):
-            signal(branch * 8 + i, 0)
-
-    def bands_below():
-        for i in range(1, 4):
-            signal(sky, i)
-
-    def enter(step):
-        if step == 0:
-            @pl.when(band != 0)
-            def _():
-                signal(sky, 0)
-        if step == 1:
-            @pl.when(inner_leader)
-            def _():
-                pl.semaphore_wait(barrier, 3)
-                signal(branch * 8, 0)
-        if step == 2:
-            @pl.when(branch_leader)
-            def _():
-                pl.semaphore_wait(barrier, 10)
-                signal(0, 0)
-        if step == 3:
-            @pl.when(root)
-            def _():
-                pl.semaphore_wait(barrier, 13)
-                for i in range(1, 4):
-                    signal(8 * i, 0)
-                leaders_below()
-                bands_below()
-        if step == 4:
-            @pl.when(branch_leader)
-            def _():
-                pl.semaphore_wait(barrier, 1)
-                leaders_below()
-                bands_below()
-        if step == 5:
-            @pl.when(inner_leader)
-            def _():
-                pl.semaphore_wait(barrier, 1)
-                bands_below()
-        if step == 6:
-            @pl.when(band != 0)
-            def _():
-                pl.semaphore_wait(barrier, 1)
-
-    enter(0)
+    def greet(i, carry):
+        row = lax.rem(sky + i, 32)
+        for column in bands:
+            pl.semaphore_signal(barrier, inc=1, device_id=(row, column), device_id_type=MESH)
+        return carry
+
+    for column in others:
+        pl.semaphore_signal(barrier, inc=1, device_id=(sky, column), device_id_type=MESH)
+    lax.fori_loop(1, 32, greet, 0)
 
     flip = reversal()
     for copy in small:
@@ -191,7 +142,6 @@
         turned = mm(maps[:, block * QUARTER:(block + 1) * QUARTER], flip, NN, lax.Precision.HIGHEST)
         xr[6 - 2 * block] = turned[:, 0:128]
         xr[7 - 2 * block] = turned[:, 128:256]
-    enter(1)
     inner, outer = order_rows()
     lane4 = lax.broadcasted_iota(jnp.int32, (BPD, 128), 1)
     pixel = lax.broadcasted_iota(jnp.int32, (BPD, QUARTER), 1)
@@ -226,7 +176,6 @@
         tp[r, 32:64, :] = sin_p
         th[r] = jnp.concatenate([ch, sh], axis=1)
         tl[r] = jnp.concatenate([cl, sl], axis=1)
-        cqh, cql, sqh, sql = [jnp.concatenate([v] * 4, axis=0) for v in (ch, cl, sh, sl)]
 
         def rows(pair, table):
             pieces = []
@@ -234,26 +183,20 @@
                 for c in range(4):
                     source = pair[c % 2][b:b + 1]
                     pieces.append(jnp.broadcast_to(source, (8, QUARTER)) * table[c * 8:c * 8 + 8])
-            return split(jnp.concatenate(pieces, axis=0))
-
-        ech, ecl = rows(even, cos_p)
-        esh, esl = rows(even, -sin_p)
-        och, ocl = rows(odd, -cos_p)
-        osh, osl = rows(odd, -sin_p)
-        right_c = jnp.concatenate([cqh, cql, cqh], axis=1)
-        right_s = jnp.concatenate([sqh, sql, sqh], axis=1)
-        real = mm(jnp.concatenate([ech, ech, ecl], axis=1), right_c, NT) + mm(
-            jnp.concatenate([esh, esh, esl], axis=1), right_s, NT
-        )
-        imag = mm(jnp.concatenate([och, och, ocl], axis=1), right_s, NT) + mm(
-            jnp.concatenate([osh, osh, osl], axis=1), right_c, NT
+            return pieces
+
+        minus_sin = -sin_p
+        by_cos = split(jnp.concatenate(rows(even, cos_p) + rows(odd, minus_sin), axis=0))
+        by_sin = split(jnp.concatenate(rows(even, minus_sin) + rows(odd, -cos_p), axis=0))
+        product = mm(
+            jnp.concatenate([by_cos[0], by_cos[0], by_cos[1]], axis=1), jnp.concatenate([ch, cl, ch], axis=1), NT
+        ) + mm(
+            jnp.concatenate([by_sin[0], by_sin[0], by_sin[1]], axis=1), jnp.concatenate([sh, sl, sh], axis=1), NT
         )
         for b in range(BPD):
-            for half, val in enumerate((real, imag)):
-                v = [val[b * 32 + c * 8:b * 32 + c * 8 + 8] for c in range(4)]
-                picked = jnp.where(
-                    quad_group == 0, v[0], jnp.where(quad_group == 1, v[1], jnp.where(quad_group == 2, v[2], v[3]))
-                )
+            for half in range(2):
+                base = half * 128 + b * 32
+                picked = jnp.concatenate([product[base + c * 8:base + c * 8 + 8] for c in range(4)], axis=1)
                 at = pl.multiple_of(((b * 2 + half) * RPD + r) * 8, 8)
                 cs[pl.ds(at, 8), :] = picked
         return carry
@@ -261,8 +204,6 @@
     def analyse_four(i, carry):
         for j in range(4):
             analyse(4 * i + j, carry)
-        for step in range(4):
-            pl.when(i == step)(functools.partial(enter, step + 2))
         return carry
 
     lax.fori_loop(0, RPD // 4, analyse_four, 0)
@@ -302,18 +243,17 @@
             send(src, dst, phase, twin, column)
         pl.when(twin != sky)(lambda: send(src, dst, phase, twin, band))
 
-    enter(6)
-
-    def slot_block(i, carry):
-        block = lax.rem(sky // 4 + i, 8)
-        at = pl.multiple_of(block * 128, 128)
-        moved = mm(hot[pl.ds(at, 128), :], flat_ref[...], NT)
-        msg[pl.ds(pl.multiple_of(block * 16, 16), 16)] = moved.reshape(16, SLOTS, 128).astype(BF)
-        send_rows(msg, arrived, 0, block * 4, 4, lax.rem(sky, 4))
+    pl.semaphore_wait(barrier, NDEV - 1)
+
+    def slot_half(i, carry):
+        half = lax.rem(sky + i, 2)
+        moved = mm(hot[pl.ds(pl.multiple_of(half * 512, 512), 512), :], flat_ref[...], NT)
+        msg[pl.ds(pl.multiple_of(half * 64, 64), 64)] = moved.reshape(64, SLOTS, 128).astype(BF)
+        send_rows(msg, arrived, 0, half * 16, 16, lax.rem(sky, 16))
         return carry
 
     flat_ref[...] = flat
-    lax.fori_loop(0, 8, slot_block, 0)
+    lax.fori_loop(0, 2, slot_half, 0)
     own = pltpu.make_async_copy(msg.at[me], arrived.at[me], local_sem)
     own.start()
     out_copies = sent(msg, arrived, 0)
@@ -372,17 +312,34 @@
     turned = jnp.concatenate(
         [returned[d * 16:d * 16 + 16].astype(F32).reshape(128, 128).T for d in range(8)], axis=1
     )
-    stacked = jnp.concatenate(split(turned), axis=0)
+    stacked = turned.astype(BF)
     lane1 = lax.broadcasted_iota(jnp.int32, (128, 128), 1)
     for pair in range(4):
         moved = mm(stacked, hot[:, pair * QUARTER:(pair + 1) * QUARTER], NN)
-        natural = (moved[0:128] + moved[128:256]) * (2.0 / math.sqrt(M))
         for half in range(2):
             a = pair * 2 + half
-            val = natural[:, half * 128:half * 128 + 128]
+            val = moved[:, half * 128:half * 128 + 128]
             if a == 0:
                 val = jnp.where(lane1 == 0, 0.5 * val, val)
             cs[pl.ds(a, 128, stride=8), :] = val
+    sub = lax.broadcasted_iota(jnp.int32, (8, QUARTER), 0)
+
+    pixel8 = lax.broadcasted_iota(jnp.int32, (8, QUARTER), 1)
+
+    def row_sums(vals):
+        for bit in (4, 2, 1):
+            low = (sub // bit) % 2 == 0
+            merged = []
+            for i in range(bit):
+                a, b = vals[i], vals[i + bit]
+                if bit == 4:
+                    merged.append(jnp.where(low, a, b) + pltpu.roll(jnp.where(low, b, a), 4, 0))
+                else:
+                    here = jnp.where(low, a, b)
+                    there = jnp.where(low, b, a)
+                    merged.append(here + jnp.where(low, pltpu.roll(there, 8 - bit, 0), pltpu.roll(there, bit, 0)))
+            vals = merged
+        return vals[0]
 
     def cycle(r):
         cos_p = tp[r, 0:32, :]
@@ -395,10 +352,8 @@
             v = cs[pl.ds(at, 8), :]
             for c in range(4):
                 pieces.append(jnp.where(quad_group == c, v, 0.0))
-        hi, lo = split(jnp.concatenate(pieces, axis=0))
-        full = mm(jnp.concatenate([hi, lo], axis=1), jnp.concatenate([table_hi, table_hi], axis=0), NN) + mm(
-            hi, table_lo, NN
-        )
+        hi = jnp.concatenate(pieces, axis=0).astype(BF)
+        full = mm(jnp.concatenate([hi, hi], axis=1), jnp.concatenate([table_hi, table_lo], axis=0), NN)
         quarters = [[], [], [], []]
         for b in range(BPD):
             re = full[(2 * b) * 32:(2 * b) * 32 + 32]
@@ -407,10 +362,13 @@
             odd = cos_p * im[:, QUARTER:] + sin_p * im[:, :QUARTER]
             ce, co = even[0:8] + even[16:24], even[8:16] + even[24:32]
             de, do = odd[0:8] + odd[16:24], odd[8:16] + odd[24:32]
-            for i, total in enumerate((ce + co - de - do, ce - co + de - do, ce - co - de + do, ce + co + de + do)):
-                quarters[i].append(jnp.sum(total, axis=0, keepdims=True))
-        inside = pixel < length_of[r] // 4
-        return [jnp.where(inside, jnp.concatenate(q, axis=0), 0.0).astype(BF).astype(F32) for q in quarters]
+            for i, total in enumerate((ce + co - de - do, ce - co - de + do, ce - co + de - do, ce + co + de + do)):
+                quarters[i].append(total)
+        inside = pixel8 < length_of[r] // 4
+        return [
+            jnp.where(inside, row_sums(q) * (2.0 / math.sqrt(M)), 0.0).astype(BF).astype(F32)
+            for q in (quarters[0] + quarters[1], quarters[2] + quarters[3])
+        ]
 
     def pixel_copy(d, i):
         return pltpu.make_async_remote_copy(
@@ -427,13 +385,13 @@
     def pixels_of(d):
         cycles = [cycle(d * DOM + k) for k in range(DOM)]
         turned = mm(
-            jnp.concatenate([q[i] for i in (1, 3) for q in cycles], axis=0).astype(BF), flip16, NN
+            jnp.concatenate([q[1] for q in cycles], axis=0).astype(BF), flip16, NN
         )
         columns = [[] for _ in range(8)]
         for k in range(DOM):
             length = length_of[d * DOM + k]
             tiles = []
-            vals = (turned[k * 4:k * 4 + 4], cycles[k][2], turned[16 + k * 4:16 + k * 4 + 4])
+            vals = (turned[k * 8:k * 8 + 4], cycles[k][0][4:8], turned[k * 8 + 4:k * 8 + 8])
             for i, offset in enumerate((length // 2 - QUARTER, length // 2, length - QUARTER)):
                 tile = (offset + 1024) // 128 - 8
                 rest = offset - tile * 128
@@ -447,7 +405,7 @@
             for t in range(8):
                 total = pb[k, 0, 8 + t - tiles[0]] + pb[k, 1, 8 + t - tiles[1]] + pb[k, 2, 8 + t - tiles[2]]
                 if t < 2:
-                    total = total + cycles[k][0][:, t * 128:t * 128 + 128]
+                    total = total + cycles[k][0][0:4, t * 128:t * 128 + 128]
                 columns[t].append(total)
         for t in range(4):
             ndb[d, t] = jnp.concatenate(
@@ -473,12 +431,12 @@
 
     def domain(d, carry):
         pixels_of(d)
-        pl.when(d > 0)(lambda: gram_of(d - 1))
         return carry
 
     lax.fori_loop(0, 4, domain, 0)
 
-    gram_of(3)
+    for d in range(4):
+        gram_of(d)
     row = lax.broadcasted_iota(jnp.int32, (BANDS, 128), 0)
     col = lax.broadcasted_iota(jnp.int32, (BANDS, 128), 1)
     systems = []
@@ -502,11 +460,8 @@
         weights = solved / jnp.sum(solved, axis=0, keepdims=True)
         for k in range(DOM):
             at = d * DOM + k
-            terms = [weights * wide[d, k, half] for half in range(2)]
-            for ref, first in ((low_ref, 0), (high_ref, 8)):
-                ref[at:at + 1, :] = jnp.concatenate(
-                    [jnp.sum(v[first:first + 8], axis=0, keepdims=True) for v in terms], axis=1
-                )
+            clean = [jnp.sum(weights * wide[d, k, half], axis=0, keepdims=True) for half in range(2)]
+            out_ref[at:at + 1, :] = jnp.concatenate(clean, axis=1)
     out_copies.wait_send()
     back_copies.wait_send()
     for d in range(4):
@@ -519,11 +474,11 @@
     whole = pl.BlockSpec(memory_space=pl.ANY)
     vmem = pltpu.VMEM
     dma = pltpu.SemaphoreType.DMA
-    low, high = pl.pallas_call(
+    return pl.pallas_call(
         whole_kernel,
-        out_shape=[jax.ShapeDtypeStruct((RPD, QUARTER), F32)] * 2,
+        out_shape=jax.ShapeDtypeStruct((RPD, QUARTER), F32),
         in_specs=[whole] * 7,
-        out_specs=[pl.BlockSpec(memory_space=vmem)] * 2,
+        out_specs=pl.BlockSpec(memory_space=vmem),
         scratch_shapes=[
             vmem((BPD * RPD, 4 * QUARTER), F32),
             pltpu.SMEM((RPD,), F32),
@@ -571,7 +526,6 @@
         band_maps.reshape(BPD * RPD, 4 * QUARTER), cycle_weight, cycle_len, m_order, m_order.reshape(8, 128),
         legendre, band_start,
     )
-    return low + high
 
 
 def solution(mesh):

time: 57.1 us -> 48.7 us (0.85)
  Pallas kernels: 54.9 us -> 46.5 us
  other arithmetic: 1.34 us -> 0 us
  local copies, waits for them, and re-layouts: 0 us -> 1.32 us
    pallas_call x1, Pallas kernels: 54.9 us -> 46.5 us  [on_device(): pl.pallas_call(whole_kernel, out_shape=jax.ShapeDtypeStruct((RPD, QUARTER...]
    add x1 -> x0, other arithmetic: 1.34 us -> none  [on_device(): return low + high]
    unnamed x0 -> x1, local copies, waits for them, and re-layouts: none -> 1.32 us
where the time goes in v3:
time: 48.7 us; the launch traced here: 48.5 us
  Pallas kernels  46.5 us (95%)
  local copies, waits for them, and re-layouts  1.32 us (3%)
  between operations  0.66 us (1%)
    pallas_call x1, Pallas kernels, on_device(): pl.pallas_call(whole_kernel, out_shape=jax.ShapeDtypeStruct((RPD, QUARTER...  46.5 us
    unnamed x1, local copies, waits for them, and re-layouts  1.32 us

profile of v3, /device:TPU:0, one launch (start us, length us, event | category | flops | bytes accessed | tf_op | source)
XLA Modules:
  0.0 48.5 jit_solution(11900521612060394205)
XLA Ops:
  0.7 46.5 %needlet_ilc.1 = f32[16,256]{1,0:T(8,128)} custom-call(f32[64,1024]{1,0:T(8,128)} %bitcast.2, f32[16]{0:T(128)} %weight_hbm.1, s32[16]{0:T(128)} %len_hbm.1, s32[1024]{0:T(1024)} %order_hbm.1, s32[8,128]{1,0:T(8,128)} %bitcast.3, bf16[8,1024,512]{2,1,0:T(8,128)(2,1)} %leg_hbm.1, s32[1]{0:T(128)S(6)} %copy.8.start_hbm), custom_call_target="tpu_custom_call" | custom-call | tf_op jit(solution)/shard_map/needlet_ilc/pallas_call | solution.py:477
  47.2 1.3 %copy.9 = f32[16,256]{1,0:T(8,128)} copy(f32[16,256]{1,0:T(8,128)} %needlet_ilc.1) | data formatting | bytes 32768

commit v4 on v3

--- a/solution.py
+++ b/solution.py
@@ -92,6 +92,11 @@
     return rows
 
 
+def k_reach(chip, reach):
+    k, j, x = chip
+    return 1 - k + reach[j] + reach[x]
+
+
 def whole_kernel(
     maps_hbm, weight_hbm, len_hbm, order_hbm, order_rows_hbm, leg_hbm, start_hbm, out_ref,
     maps, weight, length_of, order, order_vec, start, leg,
@@ -102,8 +107,10 @@
     sky = lax.axis_index("sky")
     band = lax.axis_index("band")
     me = sky * 4 + band
-    bands = [band] + [lax.rem(band + j, 4) for j in range(1, 4)]
-    others = bands[1:]
+    bands = [lax.rem(band + j, 4) for j in range(4)]
+    others = [bands[2], bands[1], bands[3]]
+    core = lax.rem(sky, 2)
+    layers = [lax.rem(sky // 2 + j, 4) for j in range(4)]
 
     small = [
         pltpu.make_async_copy(src, dst, small_sem.at[i])
@@ -120,15 +127,33 @@
 
     barrier = pltpu.get_barrier_semaphore()
 
-    def greet(i, carry):
-        row = lax.rem(sky + i, 32)
-        for column in bands:
-            pl.semaphore_signal(barrier, inc=1, device_id=(row, column), device_id_type=MESH)
-        return carry
-
-    for column in others:
-        pl.semaphore_signal(barrier, inc=1, device_id=(sky, column), device_id_type=MESH)
-    lax.fori_loop(1, 32, greet, 0)
+    group = sky // 4
+    leader = (lax.rem(sky, 4) == 0) & (band == 0)
+    root = (sky == 0) & (band == 0)
+    branch = leader & (sky != 0)
+
+    def signal(row, column):
+        pl.semaphore_signal(barrier, inc=1, device_id=(row, column), device_id_type=MESH)
+
+    def members():
+        for i in range(1, 16):
+            signal(group * 4 + i // 4, i % 4)
+
+    def climb():
+        pl.semaphore_wait(barrier, 15)
+        signal(0, 0)
+
+    def turn():
+        pl.semaphore_wait(barrier, 22)
+        for i in range(1, 8):
+            signal(4 * i, 0)
+        members()
+
+    def descend():
+        pl.semaphore_wait(barrier, 1)
+        members()
+
+    pl.when(jnp.logical_not(leader))(lambda: signal(group * 4, 0))
 
     flip = reversal()
     for copy in small:
@@ -204,6 +229,9 @@
     def analyse_four(i, carry):
         for j in range(4):
             analyse(4 * i + j, carry)
+        pl.when(branch & (i == 0))(climb)
+        pl.when(root & (i == 1))(turn)
+        pl.when(branch & (i == 2))(descend)
         return carry
 
     lax.fori_loop(0, RPD // 4, analyse_four, 0)
@@ -230,26 +258,35 @@
             recv_sem=recv_sem.at[phase], device_id=(sky, others[0]), device_id_type=MESH,
         )
 
-    def send_rows(src, dst, phase, base, count, here):
-        def rows(i, carry):
-            row = base + lax.rem(here + i, count)
-            for column in bands:
-                send(src, dst, phase, row, column)
-            return carry
-
-        lax.fori_loop(1, count, rows, 0)
-        twin = base + here
-        for column in others:
-            send(src, dst, phase, twin, column)
-        pl.when(twin != sky)(lambda: send(src, dst, phase, twin, band))
-
-    pl.semaphore_wait(barrier, NDEV - 1)
+    reach = {0: 0, 1: 1, 2: 2, 3: 1}
+    chips = sorted(
+        ((k, j, x) for k in range(2) for j in range(4) for x in range(4)),
+        key=lambda c: k_reach(c, reach), reverse=True,
+    )
+
+    def half_of(i):
+        return lax.rem(sky // 16 + 1 + i, 2)
+
+    def send_half(src, dst, phase, i):
+        half = half_of(i)
+        same = half * 2 + lax.rem(sky // 8, 2)
+        beside = half * 2 + 1 - lax.rem(sky // 8, 2)
+        planes = [jnp.where(i == 0, same, beside), jnp.where(i == 0, beside, same)]
+        for k, j, x in chips:
+            row = planes[k] * 8 + layers[j] * 2
+            send(src, dst, phase, row + 1 - core, bands[x])
+            if (k, j, x) == (1, 0, 0):
+                pl.when(i == 0)(lambda: send(src, dst, phase, row + core, bands[x]))
+            else:
+                send(src, dst, phase, row + core, bands[x])
+
+    pl.when(jnp.logical_not(leader))(lambda: pl.semaphore_wait(barrier, 1))
 
     def slot_half(i, carry):
-        half = lax.rem(sky + i, 2)
+        half = half_of(i)
         moved = mm(hot[pl.ds(pl.multiple_of(half * 512, 512), 512), :], flat_ref[...], NT)
         msg[pl.ds(pl.multiple_of(half * 64, 64), 64)] = moved.reshape(64, SLOTS, 128).astype(BF)
-        send_rows(msg, arrived, 0, half * 16, 16, lax.rem(sky, 16))
+        send_half(msg, arrived, 0, i)
         return carry
 
     flat_ref[...] = flat
@@ -279,7 +316,7 @@
         filtered[m] = (mm(coeff, leg[m], NT) * keep).astype(BF)
 
     def cycle_half(i, carry):
-        half = lax.rem(sky + i, 2)
+        half = half_of(i)
         at = pl.multiple_of(half * QUARTER, QUARTER)
         for m in range(SLOTS):
             result = mm(filtered[m], leg[m, :, pl.ds(at, QUARTER)], NN)
@@ -293,7 +330,7 @@
                     done.append(hy[side, row:row + 8, :])
                 for k, val in enumerate(swap_blocks(done, lane_group)):
                     back[(half * 16 + side * 8 + k) * 4 + source] = val.astype(back.dtype)
-        send_rows(back, returned, 1, half * 16, 16, lax.rem(sky, 16))
+        send_half(back, returned, 1, i)
         return carry
 
     lax.fori_loop(0, 2, cycle_half, 0)

time: 48.7 us -> 49.4 us (1.014)
  Pallas kernels: 46.5 us -> 47.3 us
    pallas_call x1, Pallas kernels: 46.5 us -> 47.3 us  [on_device(): pl.pallas_call(whole_kernel, out_shape=jax.ShapeDtypeStruct((RPD, QUARTER...]
where the time goes in v4:
time: 49.4 us; the launch traced here: 49.3 us
  Pallas kernels  47.3 us (96%)
  local copies, waits for them, and re-layouts  1.32 us (3%)
  between operations  0.66 us (1%)
    pallas_call x1, Pallas kernels, on_device(): pl.pallas_call(whole_kernel, out_shape=jax.ShapeDtypeStruct((RPD, QUARTER...  47.3 us
    unnamed x1, local copies, waits for them, and re-layouts  1.32 us

profile of v4, /device:TPU:0, one launch (start us, length us, event | category | flops | bytes accessed | tf_op | source)
XLA Modules:
  0.0 49.3 jit_solution(17171582135678881732)
XLA Ops:
  0.7 47.3 %needlet_ilc.1 = f32[16,256]{1,0:T(8,128)} custom-call(f32[64,1024]{1,0:T(8,128)} %bitcast.2, f32[16]{0:T(128)} %weight_hbm.1, s32[16]{0:T(128)} %len_hbm.1, s32[1024]{0:T(1024)} %order_hbm.1, s32[8,128]{1,0:T(8,128)} %bitcast.3, bf16[8,1024,512]{2,1,0:T(8,128)(2,1)} %leg_hbm.1, s32[1]{0:T(128)S(6)} %copy.8.start_hbm), custom_call_target="tpu_custom_call" | custom-call | tf_op jit(solution)/shard_map/needlet_ilc/pallas_call | solution.py:514
  47.9 1.3 %copy.9 = f32[16,256]{1,0:T(8,128)} copy(f32[16,256]{1,0:T(8,128)} %needlet_ilc.1) | data formatting | bytes 32768

commit v5 on v4

--- a/solution.py
+++ b/solution.py
@@ -15,6 +15,7 @@
 RIDGE = 0.05
 QUARTER = 256
 NDEV = 128
+HALF = 64
 BPD = 4
 RPD = 16
 GROUPS = 2 * BPD
@@ -100,7 +101,7 @@
 def whole_kernel(
     maps_hbm, weight_hbm, len_hbm, order_hbm, order_rows_hbm, leg_hbm, start_hbm, out_ref,
     maps, weight, length_of, order, order_vec, start, leg,
-    xs, xr, cs, tp, th, tl, hot, flat_ref, msg, arrived, hx, hy, filtered, back, returned, pb, ndb, got, wide,
+    xs, xr, cs, tp, th, tl, hot, flat_ref, msg, arrived, hx, hy, partial, filtered, early, back, returned, pb, ndb, got, wide,
     part, parts,
     small_sem, leg_sem, local_sem, send_sem, recv_sem, pix_send, pix_recv, cov_send, cov_recv,
 ):
@@ -127,33 +128,15 @@
 
     barrier = pltpu.get_barrier_semaphore()
 
-    group = sky // 4
-    leader = (lax.rem(sky, 4) == 0) & (band == 0)
-    root = (sky == 0) & (band == 0)
-    branch = leader & (sky != 0)
-
-    def signal(row, column):
-        pl.semaphore_signal(barrier, inc=1, device_id=(row, column), device_id_type=MESH)
-
-    def members():
-        for i in range(1, 16):
-            signal(group * 4 + i // 4, i % 4)
-
-    def climb():
-        pl.semaphore_wait(barrier, 15)
-        signal(0, 0)
-
-    def turn():
-        pl.semaphore_wait(barrier, 22)
-        for i in range(1, 8):
-            signal(4 * i, 0)
-        members()
-
-    def descend():
-        pl.semaphore_wait(barrier, 1)
-        members()
-
-    pl.when(jnp.logical_not(leader))(lambda: signal(group * 4, 0))
+    def greet(i, carry):
+        row = lax.rem(sky + i, 32)
+        for column in bands:
+            pl.semaphore_signal(barrier, inc=1, device_id=(row, column), device_id_type=MESH)
+        return carry
+
+    for column in others:
+        pl.semaphore_signal(barrier, inc=1, device_id=(sky, column), device_id_type=MESH)
+    lax.fori_loop(1, 32, greet, 0)
 
     flip = reversal()
     for copy in small:
@@ -229,9 +212,6 @@
     def analyse_four(i, carry):
         for j in range(4):
             analyse(4 * i + j, carry)
-        pl.when(branch & (i == 0))(climb)
-        pl.when(root & (i == 1))(turn)
-        pl.when(branch & (i == 2))(descend)
         return carry
 
     lax.fori_loop(0, RPD // 4, analyse_four, 0)
@@ -246,16 +226,16 @@
             [jnp.where(target == lane128 + 128.0 * a, 1.0, 0.0).astype(BF) for a in range(8)], axis=1
         )
 
-    def send(src, dst, phase, row, column):
+    def send(src, dst, phase, i, row, column):
         pltpu.make_async_remote_copy(
             src_ref=src.at[row * 4 + column], dst_ref=dst.at[me], send_sem=send_sem.at[phase],
-            recv_sem=recv_sem.at[phase], device_id=(row, column), device_id_type=MESH,
+            recv_sem=recv_sem.at[phase, i], device_id=(row, column), device_id_type=MESH,
         ).start()
 
-    def sent(src, dst, phase):
+    def sent(src, dst, phase, i, count):
         return pltpu.make_async_remote_copy(
-            src_ref=src.at[pl.ds(0, NDEV - 1)], dst_ref=dst.at[pl.ds(0, NDEV - 1)], send_sem=send_sem.at[phase],
-            recv_sem=recv_sem.at[phase], device_id=(sky, others[0]), device_id_type=MESH,
+            src_ref=src.at[pl.ds(0, count)], dst_ref=dst.at[pl.ds(0, count)], send_sem=send_sem.at[phase],
+            recv_sem=recv_sem.at[phase, i], device_id=(sky, others[0]), device_id_type=MESH,
         )
 
     reach = {0: 0, 1: 1, 2: 2, 3: 1}
@@ -274,13 +254,13 @@
         planes = [jnp.where(i == 0, same, beside), jnp.where(i == 0, beside, same)]
         for k, j, x in chips:
             row = planes[k] * 8 + layers[j] * 2
-            send(src, dst, phase, row + 1 - core, bands[x])
+            send(src, dst, phase, i, row + 1 - core, bands[x])
             if (k, j, x) == (1, 0, 0):
-                pl.when(i == 0)(lambda: send(src, dst, phase, row + core, bands[x]))
+                pl.when(i == 0)(lambda: send(src, dst, phase, i, row + core, bands[x]))
             else:
-                send(src, dst, phase, row + core, bands[x])
-
-    pl.when(jnp.logical_not(leader))(lambda: pl.semaphore_wait(barrier, 1))
+                send(src, dst, phase, i, row + core, bands[x])
+
+    pl.semaphore_wait(barrier, NDEV - 1)
 
     def slot_half(i, carry):
         half = half_of(i)
@@ -293,27 +273,34 @@
     lax.fori_loop(0, 2, slot_half, 0)
     own = pltpu.make_async_copy(msg.at[me], arrived.at[me], local_sem)
     own.start()
-    out_copies = sent(msg, arrived, 0)
     window_at = lax.broadcasted_iota(jnp.int32, (8, LB), 1).astype(F32)
     taper = window_taper(window_at)[0:1] * (1.0 / math.sqrt(LB))
     degree = lax.broadcasted_iota(jnp.int32, (1, LB), 1) + start[0]
     own.wait()
-    out_copies.wait_recv()
 
     lane_group = lax.broadcasted_iota(jnp.int32, (SLOTS, 128), 1) // 16
-    for tile in range(4):
-        for source in range(4):
-            here = [arrived[(tile * 8 + i) * 4 + source].astype(F32) for i in range(8)]
-            for g, val in enumerate(swap_blocks(here, lane_group)):
-                at = (source * GROUPS + g) * 8
-                hx[tile, at:at + 8, :] = val
-    for m in range(SLOTS):
-        keep = jnp.where(degree >= order[me * SLOTS + m], taper, 0.0)
-        coeff = jnp.concatenate(
-            [hx[tile, pl.ds(m, 4 * GROUPS, stride=8), :].astype(BF) for tile in range(4)], axis=1
-        )
-        loads[m].wait()
-        filtered[m] = (mm(coeff, leg[m], NT) * keep).astype(BF)
+    for i in range(2):
+        half = half_of(i)
+        sent(msg, arrived, 0, i, HALF - i).wait_recv()
+        for side in range(2):
+            for source in range(4):
+                here = [arrived[(half * 16 + side * 8 + k) * 4 + source].astype(F32) for k in range(8)]
+                for g, val in enumerate(swap_blocks(here, lane_group)):
+                    at = (source * GROUPS + g) * 8
+                    hx[2 * i + side, at:at + 8, :] = val
+        at = pl.multiple_of(half * QUARTER, QUARTER)
+        for m in range(SLOTS):
+            coeff = jnp.concatenate(
+                [hx[2 * i + side, pl.ds(m, 4 * GROUPS, stride=8), :].astype(BF) for side in range(2)], axis=1
+            )
+            if i == 0:
+                loads[m].wait()
+            share = mm(coeff, leg[m, :, pl.ds(at, QUARTER)], NT)
+            if i == 0:
+                partial[m] = share
+            else:
+                keep = jnp.where(degree >= order[me * SLOTS + m], taper, 0.0)
+                filtered[m] = ((partial[m] + share) * keep).astype(BF)
 
     def cycle_half(i, carry):
         half = half_of(i)
@@ -336,7 +323,6 @@
     lax.fori_loop(0, 2, cycle_half, 0)
     own_back = pltpu.make_async_copy(back.at[me], returned.at[me], local_sem)
     own_back.start()
-    back_copies = sent(back, returned, 1)
     for k in range(4):
         for i in range(3):
             for tile in range(20):
@@ -344,23 +330,29 @@
                     pb[k, i, tile] = jnp.zeros((BPD, 128), F32)
     flip16 = flip.astype(BF)
     own_back.wait()
-    back_copies.wait_recv()
-
-    turned = jnp.concatenate(
-        [returned[d * 16:d * 16 + 16].astype(F32).reshape(128, 128).T for d in range(8)], axis=1
-    )
-    stacked = turned.astype(BF)
+
     lane1 = lax.broadcasted_iota(jnp.int32, (128, 128), 1)
-    for pair in range(4):
-        moved = mm(stacked, hot[:, pair * QUARTER:(pair + 1) * QUARTER], NN)
-        for half in range(2):
-            a = pair * 2 + half
-            val = moved[:, half * 128:half * 128 + 128]
-            if a == 0:
-                val = jnp.where(lane1 == 0, 0.5 * val, val)
-            cs[pl.ds(a, 128, stride=8), :] = val
+    for i in range(2):
+        half = half_of(i)
+        sent(back, returned, 1, i, HALF - i).wait_recv()
+        turned = jnp.concatenate(
+            [returned[pl.ds(half * HALF + d * 16, 16)].astype(F32).reshape(128, 128).T for d in range(4)], axis=1
+        ).astype(BF)
+        at = half * 512
+        for pair in range(4):
+            lanes = slice(pair * QUARTER, (pair + 1) * QUARTER)
+            moved = mm(turned, hot[pl.ds(pl.multiple_of(at, 512), 512), lanes], NN)
+            if i == 0:
+                early[:, lanes] = moved
+                continue
+            moved = moved + early[:, lanes]
+            for side in range(2):
+                a = pair * 2 + side
+                val = moved[:, side * 128:side * 128 + 128]
+                if a == 0:
+                    val = jnp.where(lane1 == 0, 0.5 * val, val)
+                cs[pl.ds(a, 128, stride=8), :] = val
     sub = lax.broadcasted_iota(jnp.int32, (8, QUARTER), 0)
-
     pixel8 = lax.broadcasted_iota(jnp.int32, (8, QUARTER), 1)
 
     def row_sums(vals):
@@ -499,8 +491,9 @@
             at = d * DOM + k
             clean = [jnp.sum(weights * wide[d, k, half], axis=0, keepdims=True) for half in range(2)]
             out_ref[at:at + 1, :] = jnp.concatenate(clean, axis=1)
-    out_copies.wait_send()
-    back_copies.wait_send()
+    for i in range(2):
+        sent(msg, arrived, 0, i, HALF - i).wait_send()
+        sent(back, returned, 1, i, HALF - i).wait_send()
     for d in range(4):
         for i in range(3):
             pixel_copy(d, i).wait_send()
@@ -536,7 +529,9 @@
             vmem((NDEV, SLOTS, 128), BF),
             vmem((4, 4 * GROUPS * SLOTS, 128), F32),
             vmem((2, 4 * GROUPS * SLOTS, 128), F32),
+            vmem((SLOTS, 4 * GROUPS, LB), F32),
             vmem((SLOTS, 4 * GROUPS, LB), BF),
+            vmem((128, M), F32),
             vmem((NDEV, SLOTS, 128), BACK),
             vmem((NDEV, SLOTS, 128), BACK),
             vmem((DOM, 3, 20, BPD, 128), F32),
@@ -549,7 +544,7 @@
             dma((SLOTS,)),
             dma,
             dma((2,)),
-            dma((2,)),
+            dma((2, 2)),
             dma((4, 3)),
             dma((4, 3)),
             dma((4, 3)),

time: 49.4 us -> 46.1 us (0.933)
  Pallas kernels: 47.3 us -> 44 us
    pallas_call x1, Pallas kernels: 47.3 us -> 44 us  [on_device(): pl.pallas_call(whole_kernel, out_shape=jax.ShapeDtypeStruct((RPD, QUARTER...]
where the time goes in v5:
time: 46.1 us; the launch traced here: 46 us
  Pallas kernels  44 us (95%)
  local copies, waits for them, and re-layouts  1.32 us (3%)
  between operations  0.66 us (1%)
    pallas_call x1, Pallas kernels, on_device(): pl.pallas_call(whole_kernel, out_shape=jax.ShapeDtypeStruct((RPD, QUARTER...  44 us
    unnamed x1, local copies, waits for them, and re-layouts  1.32 us

profile of v5, /device:TPU:0, one launch (start us, length us, event | category | flops | bytes accessed | tf_op | source)
XLA Modules:
  0.0 46.0 jit_solution(13226886221766641254)
XLA Ops:
  0.7 44.0 %needlet_ilc.1 = f32[16,256]{1,0:T(8,128)} custom-call(f32[64,1024]{1,0:T(8,128)} %bitcast.2, f32[16]{0:T(128)} %weight_hbm.1, s32[16]{0:T(128)} %len_hbm.1, s32[1024]{0:T(1024)} %order_hbm.1, s32[8,128]{1,0:T(8,128)} %bitcast.3, bf16[8,1024,512]{2,1,0:T(8,128)(2,1)} %leg_hbm.1, s32[1]{0:T(128)S(6)} %copy.8.start_hbm), custom_call_target="tpu_custom_call" | custom-call | tf_op jit(solution)/shard_map/needlet_ilc/pallas_call | solution.py:507
  44.6 1.3 %copy.9 = f32[16,256]{1,0:T(8,128)} copy(f32[16,256]{1,0:T(8,128)} %needlet_ilc.1) | data formatting | bytes 32768

commit v6 on v5

--- a/solution.py
+++ b/solution.py
@@ -58,10 +58,20 @@
 
 
 def order_rows():
-    row = lax.broadcasted_iota(jnp.int32, (32, QUARTER), 0)
-    inner = (4 * (row % 8) + row // 8).astype(F32)
-    outer = (32 * row).astype(F32)
-    return inner, outer
+    row = lax.broadcasted_iota(jnp.int32, (24, QUARTER), 0)
+    small = jnp.where(row < 20, row - 16, 256 * (row - 20))
+    return jnp.where(row < 8, 4 * row, jnp.where(row < 16, 32 * (row - 8), small)).astype(F32)
+
+
+def cycle_tables(orders, length):
+    cos, sin = trig_tables(orders, length)
+    tables = []
+    for start, step in ((0, 16), (8, 20)):
+        cb, sb = cos[start:start + 8], sin[start:start + 8]
+        cs = [(cos[step + i:step + i + 1], sin[step + i:step + i + 1]) for i in range(4)]
+        tables.append(jnp.concatenate([cb * c - sb * s for c, s in cs], axis=0))
+        tables.append(jnp.concatenate([sb * c + cb * s for c, s in cs], axis=0))
+    return tables
 
 
 def reversal():
@@ -150,7 +160,7 @@
         turned = mm(maps[:, block * QUARTER:(block + 1) * QUARTER], flip, NN, lax.Precision.HIGHEST)
         xr[6 - 2 * block] = turned[:, 0:128]
         xr[7 - 2 * block] = turned[:, 128:256]
-    inner, outer = order_rows()
+    orders = order_rows()
     lane4 = lax.broadcasted_iota(jnp.int32, (BPD, 128), 1)
     pixel = lax.broadcasted_iota(jnp.int32, (BPD, QUARTER), 1)
     quad_group = lax.broadcasted_iota(jnp.int32, (8, 128), 1) // 32
@@ -176,8 +186,7 @@
         x0, x1, x2, x3 = [jnp.where(inside, v, 0.0) * scale for v in (x0, x1, x2, x3)]
         even = ((x0 + x3) + (x1 + x2), (x0 + x3) - (x1 + x2))
         odd = ((x0 - x3) - (x1 - x2), (x0 - x3) + (x1 - x2))
-        cos_p, sin_p = trig_tables(inner, length)
-        cos_q, sin_q = trig_tables(outer, length)
+        cos_p, sin_p, cos_q, sin_q = cycle_tables(orders, length)
         ch, cl = split(cos_q)
         sh, sl = split(sin_q)
         tp[r, 0:32, :] = cos_p
@@ -194,12 +203,12 @@
             return pieces
 
         minus_sin = -sin_p
-        by_cos = split(jnp.concatenate(rows(even, cos_p) + rows(odd, minus_sin), axis=0))
-        by_sin = split(jnp.concatenate(rows(even, minus_sin) + rows(odd, -cos_p), axis=0))
+        by_cos = jnp.concatenate(rows(even, cos_p) + rows(odd, minus_sin), axis=0).astype(BF)
+        by_sin = jnp.concatenate(rows(even, minus_sin) + rows(odd, -cos_p), axis=0).astype(BF)
         product = mm(
-            jnp.concatenate([by_cos[0], by_cos[0], by_cos[1]], axis=1), jnp.concatenate([ch, cl, ch], axis=1), NT
+            jnp.concatenate([by_cos, by_cos], axis=1), jnp.concatenate([ch, cl], axis=1), NT
         ) + mm(
-            jnp.concatenate([by_sin[0], by_sin[0], by_sin[1]], axis=1), jnp.concatenate([sh, sl, sh], axis=1), NT
+            jnp.concatenate([by_sin, by_sin], axis=1), jnp.concatenate([sh, sl], axis=1), NT
         )
         for b in range(BPD):
             for half in range(2):

time: 46.1 us -> 44.5 us (0.965)
  Pallas kernels: 44 us -> 42.3 us
    pallas_call x1, Pallas kernels: 44 us -> 42.3 us  [on_device(): pl.pallas_call(whole_kernel, out_shape=jax.ShapeDtypeStruct((RPD, QUARTER...]
where the time goes in v6:
time: 44.5 us; the launch traced here: 44.3 us
  Pallas kernels  42.3 us (95%)
  local copies, waits for them, and re-layouts  1.32 us (3%)
  between operations  0.66 us (1%)
    pallas_call x1, Pallas kernels, on_device(): pl.pallas_call(whole_kernel, out_shape=jax.ShapeDtypeStruct((RPD, QUARTER...  42.3 us
    unnamed x1, local copies, waits for them, and re-layouts  1.32 us

profile of v6, /device:TPU:0, one launch (start us, length us, event | category | flops | bytes accessed | tf_op | source)
XLA Modules:
  0.0 44.3 jit_solution(10589070044096589677)
XLA Ops:
  0.7 42.3 %needlet_ilc.1 = f32[16,256]{1,0:T(8,128)} custom-call(f32[64,1024]{1,0:T(8,128)} %bitcast.2, f32[16]{0:T(128)} %weight_hbm.1, s32[16]{0:T(128)} %len_hbm.1, s32[1024]{0:T(1024)} %order_hbm.1, s32[8,128]{1,0:T(8,128)} %bitcast.3, bf16[8,1024,512]{2,1,0:T(8,128)(2,1)} %leg_hbm.1, s32[1]{0:T(128)S(6)} %copy.8.start_hbm), custom_call_target="tpu_custom_call" | custom-call | tf_op jit(solution)/shard_map/needlet_ilc/pallas_call | solution.py:516
  43.0 1.3 %copy.9 = f32[16,256]{1,0:T(8,128)} copy(f32[16,256]{1,0:T(8,128)} %needlet_ilc.1) | data formatting | bytes 32768

commit v7 on v6

--- a/solution.py
+++ b/solution.py
@@ -203,12 +203,12 @@
             return pieces
 
         minus_sin = -sin_p
-        by_cos = jnp.concatenate(rows(even, cos_p) + rows(odd, minus_sin), axis=0).astype(BF)
-        by_sin = jnp.concatenate(rows(even, minus_sin) + rows(odd, -cos_p), axis=0).astype(BF)
+        by_cos = split(jnp.concatenate(rows(even, cos_p) + rows(odd, minus_sin), axis=0))
+        by_sin = split(jnp.concatenate(rows(even, minus_sin) + rows(odd, -cos_p), axis=0))
         product = mm(
-            jnp.concatenate([by_cos, by_cos], axis=1), jnp.concatenate([ch, cl], axis=1), NT
+            jnp.concatenate([by_cos[0], by_cos[0], by_cos[1]], axis=1), jnp.concatenate([ch, cl, ch], axis=1), NT
         ) + mm(
-            jnp.concatenate([by_sin, by_sin], axis=1), jnp.concatenate([sh, sl], axis=1), NT
+            jnp.concatenate([by_sin[0], by_sin[0], by_sin[1]], axis=1), jnp.concatenate([sh, sl, sh], axis=1), NT
         )
         for b in range(BPD):
             for half in range(2):
@@ -219,11 +219,11 @@
         return carry
 
     def analyse_four(i, carry):
-        for j in range(4):
-            analyse(4 * i + j, carry)
+        for j in range(8):
+            analyse(8 * i + j, carry)
         return carry
 
-    lax.fori_loop(0, RPD // 4, analyse_four, 0)
+    lax.fori_loop(0, RPD // 8, analyse_four, 0)
 
     flat = jnp.concatenate([cs[pl.ds(a, 128, stride=8), :].astype(BF) for a in range(8)], axis=1)
     slots = order_vec[...]

time: 44.5 us -> 44.9 us (level)
  no operation moved by 1% of the time
where the time goes in v7:
time: 44.9 us; the launch traced here: 44.7 us
  Pallas kernels  42.7 us (95%)
  local copies, waits for them, and re-layouts  1.32 us (3%)
  between operations  0.66 us (1%)
    pallas_call x1, Pallas kernels, on_device(): pl.pallas_call(whole_kernel, out_shape=jax.ShapeDtypeStruct((RPD, QUARTER...  42.7 us
    unnamed x1, local copies, waits for them, and re-layouts  1.32 us

profile of v7, /device:TPU:0, one launch (start us, length us, event | category | flops | bytes accessed | tf_op | source)
XLA Modules:
  0.0 44.7 jit_solution(2081413950776576301)
XLA Ops:
  0.7 42.7 %needlet_ilc.1 = f32[16,256]{1,0:T(8,128)} custom-call(f32[64,1024]{1,0:T(8,128)} %bitcast.2, f32[16]{0:T(128)} %weight_hbm.1, s32[16]{0:T(128)} %len_hbm.1, s32[1024]{0:T(1024)} %order_hbm.1, s32[8,128]{1,0:T(8,128)} %bitcast.3, bf16[8,1024,512]{2,1,0:T(8,128)(2,1)} %leg_hbm.1, s32[1]{0:T(128)S(6)} %copy.8.start_hbm), custom_call_target="tpu_custom_call" | custom-call | tf_op jit(solution)/shard_map/needlet_ilc/pallas_call | solution.py:516
  43.4 1.3 %copy.9 = f32[16,256]{1,0:T(8,128)} copy(f32[16,256]{1,0:T(8,128)} %needlet_ilc.1) | data formatting | bytes 32768
